TPU v7x, 32 devices: a whole 2x2x4 slice. The times are simulated.
32 devices in a mesh: bead: 8 (over y, x, core), space: 4 (over z).
Axes of the slice: x: 2, y: 2, z: 4, core: 2. Of those that a mesh axis runs over, the one named last changes fastest.
Arguments:
- positions: float32 [32, 3, 2048], P('bead', None, 'space'), may hold values from -3 to 3
- momenta: float32 [32, 3, 2048], P('bead', None, 'space'), may hold values from -6 to 6
- neighbours: int32 [32, 2048], P(None, 'space'), may hold values from 0 to 767, as said below
- ghost_rows: int32 [1024], P('space'), may hold values from 0 to 511
- species: int32 [2048], P('space'), may hold values from 0 to 1
- species_scale: float32 [2], replicated, may hold values from 0.5 to 2
- mass_table: float32 [2], replicated, may hold values from 0.25 to 1
- w_in: float32 [128, 8], replicated, may hold values from -2 to 2
- w_out: float32 [8, 128], replicated, may hold values from -0.5 to 0.5
Outputs:
- new_positions: float32 [32, 3, 2048], P('bead', None, 'space')
- new_momenta: float32 [32, 3, 2048], P('bead', None, 'space')
Inputs may be any that keep to these rules, and one draw needn't show every extreme that they name: `neighbours`: A neighbour entry indexes the window of its atom's domain; slots beyond an atom's live count hold the atom's own position 128 + (atom index mod 512); every atom has at least 8 live slots. `ghost_rows`: domain d's block is entries 2 * 128 * d to 2 * 128 * (d + 1) - 1; entries index atoms within domain d.
All inputs are finite; a program needn't handle non-finite values.
Results may differ from a plain program's by a relative error of at most 0.0003.
Values sent between devices are 32-bit elements; how exact they have to be, the bound alone decides.
A program may use at most 64 MiB of HBM per device.

v0:
```python
import jax
import jax.numpy as jnp
import numpy as np
from jax import lax
from jax.experimental import pallas as pl
from jax.experimental.pallas import tpu as pltpu
from jax.sharding import PartitionSpec as P

BEADS = 32
CB = 4
NINNER = 3


polymer_freq = 10.0
outer_step = 6.0
pair_width = 1.0
pair_strength = 1.0
highest = lax.Precision.HIGHEST


def mode_matrix(count):
    beadpos = np.arange(count)[None, :]
    modeidx = np.arange(count)[:, None]
    middle = count // 2
    cosine = np.sqrt(2.0 / count) * np.cos(2.0 * np.pi * beadpos * modeidx / count)
    sine_rows = np.sqrt(2.0 / count) * np.sin(2.0 * np.pi * beadpos * modeidx / count)
    matrix = np.where(modeidx < middle, cosine, sine_rows)
    matrix = np.where(modeidx == 0, 1.0 / np.sqrt(count), matrix)
    matrix = np.where(modeidx == middle, np.cos(np.pi * beadpos) / np.sqrt(count), matrix)
    return matrix


def mode_scales(count, inner_step):
    frequency = 2.0 * polymer_freq * np.sin(np.pi * np.arange(count) / count)
    nonzero = np.where(frequency > 0, frequency, 1.0)
    cosine = np.cos(frequency * inner_step)
    drift_gain = np.where(frequency > 0, np.sin(frequency * inner_step) / nonzero, inner_step)
    spring = frequency * np.sin(frequency * inner_step)
    return (cosine, drift_gain, spring)


def contraction(count, fewer):
    full_modes = mode_matrix(count)
    small_modes = mode_matrix(fewer)
    kept = list(range(fewer // 2 + 1)) + list(range(count - fewer // 2 + 1, count))
    contract = np.sqrt(fewer / count) * (small_modes.T @ full_modes[kept])
    expand = count / fewer * contract.T
    return (contract, expand)


def radial_rates(count):
    return 0.2 * 2.0 ** (np.arange(count) / 2.0)

LANES = 128
TILE = 8
MESH = pl.DeviceIdType.MESH


def tables(devices, per_device):
    inner_step = outer_step / NINNER
    modes = mode_matrix(BEADS)
    cosine, drift_gain, spring = mode_scales(BEADS, inner_step)
    persist = modes.T @ (cosine[:, None] * modes)
    coupling = modes.T @ (drift_gain[:, None] * modes)
    restoring = -(modes.T @ (spring[:, None] * modes))
    contract, expand = contraction(BEADS, CB)
    rows = -(-6 * per_device // TILE) * TILE
    full = devices * rows
    blocks = ((persist, coupling), (restoring, persist))

    def places(component, kind):
        bead = np.arange(BEADS)
        local = component * 2 * per_device + kind * per_device + bead % per_device
        return bead // per_device * rows + local

    move = np.zeros((full, full))
    reduce = np.zeros((CB, TILE, full))
    spread = np.zeros((full, CB * TILE))
    for component in range(3):
        for out in range(2):
            for kind in range(2):
                move[np.ix_(places(component, out), places(component, kind))] = blocks[out][kind]
        for member in range(CB):
            reduce[member, component, places(component, 0)] = contract[member]
            spread[places(component, 1), member * TILE + component] = (
                0.5 * outer_step * expand[:, member]
            )
    reduce_moved = np.repeat(reduce @ move, devices // CB, axis=0)
    move_spread = (move @ spread).reshape(devices, rows, CB * TILE)
    share = reduce.reshape(CB * TILE, devices, rows).transpose(1, 0, 2)
    spread = spread.reshape(devices, rows, CB * TILE)
    move = np.concatenate((move.reshape(devices, rows, full), move_spread), axis=2)

    def padded(table):
        return np.pad(table, ((0, 0), (0, 0), (0, move.shape[2] - table.shape[2])))

    stacked = (move, padded(reduce_moved), padded(spread), padded(share))
    return jnp.asarray(np.concatenate(stacked, axis=1), jnp.float32)


def dot(a, b):
    return jnp.dot(a, b, precision=highest, preferred_element_type=jnp.float32)


def pick(chunks, low, high):
    found = None
    for number, chunk in enumerate(chunks):
        value = jnp.take_along_axis(chunk, low, axis=1, mode="promise_in_bounds")
        found = value if found is None else jnp.where(high == number, value, found)
    return found


def cycle_kernel(
    pos_in, mom_in, near_in, ghost_from, species_in, scale_in, mass_in, w_in_in, w_out_in, table_in,
    new_pos_ref, new_mom_ref,
    state, kick, weight, gathered, ghost_out, ghost_in, part_out, part_in, whole,
    qghost_out, qghost_in, piece, edge_out, edge_in,
    pos_ref, mom_ref, near_ref, ghost_ref, species_ref, scale_ref, mass_ref, w_in_ref, w_out_ref,
    table_ref, load_s, edge_s, edge_r,
    part_s, part_r, ghost_s, ghost_r, qghost_s, qghost_r, all_s, all_r, piece_s, piece_r,
):
    _, per_device, atoms = pos_ref.shape
    slots = near_ref.shape[0]
    rows = state.shape[1]
    ghosts = ghost_ref.shape[1]
    devices = lax.axis_size("bead")
    domains = lax.axis_size("space")
    me = lax.axis_index("bead")
    domain = lax.axis_index("space")
    above = lax.rem(domain + 1, domains)
    below = lax.rem(domain + domains - 1, domains)
    peers = [lax.rem(me + j, devices) for j in range(devices)]
    senders = [lax.rem(me + devices - j, devices) for j in range(devices)]
    inner_step = outer_step / NINNER
    groups = devices // CB
    share = atoms // groups
    cover = piece.shape[3]
    member = me // groups
    first = lax.rem(me, groups) * share // LANES * LANES
    ghost_chunks = ghosts // LANES
    atom_chunks = atoms // LANES

    loads = [
        pltpu.make_async_copy(src, dst, load_s.at[number])
        for number, (src, dst) in enumerate((
            (pos_in, pos_ref), (mom_in, mom_ref), (species_in, species_ref), (scale_in, scale_ref),
            (mass_in, mass_ref), (table_in.at[me], table_ref), (ghost_from, ghost_ref),
            (near_in, near_ref), (w_in_in, w_in_ref), (w_out_in, w_out_ref),
        ))
    ]
    for load in loads:
        load.start()
    barrier = pltpu.get_barrier_semaphore()
    for j in range(1, devices):
        pl.semaphore_signal(barrier, inc=1, device_id={"bead": peers[j]}, device_id_type=MESH)
    for target in (above, below):
        for j in range(devices):
            pl.semaphore_signal(
                barrier, inc=1, device_id={"bead": peers[j], "space": target}, device_id_type=MESH
            )

    def to_peer(src, dst, send, recv, j):
        return pltpu.make_async_remote_copy(
            src_ref=src, dst_ref=dst, send_sem=send.at[j], recv_sem=recv.at[j],
            device_id={"bead": peers[j]}, device_id_type=MESH,
        )

    def to_side(src, dst, send, recv, side):
        return pltpu.make_async_remote_copy(
            src_ref=src, dst_ref=dst, send_sem=send.at[side], recv_sem=recv.at[side],
            device_id={"space": (above, below)[side]}, device_id_type=MESH,
        )

    def to_edge(step, side, j):
        return pltpu.make_async_remote_copy(
            src_ref=edge_out.at[step, side], dst_ref=edge_in.at[step, side, me],
            send_sem=edge_s.at[step, side, j], recv_sem=edge_r.at[step, side, j],
            device_id={"bead": peers[j], "space": (above, below)[side]}, device_id_type=MESH,
        )

    def await_edges(step):
        for side in range(2):
            for j in range(devices):
                pltpu.make_async_remote_copy(
                    src_ref=edge_out.at[step, side], dst_ref=edge_in.at[step, side, senders[j]],
                    send_sem=edge_s.at[step, side, j], recv_sem=edge_r.at[step, side, j],
                    device_id={"bead": peers[j], "space": (above, below)[side]},
                    device_id_type=MESH,
                ).wait_recv()

    def row_of(component, kind, bead):
        return (component * 2 + kind) * per_device + bead

    full = devices * rows
    moved_row = rows
    spread_row_at = moved_row + TILE
    share_row = spread_row_at + rows
    for load in loads:
        load.wait()
    species = species_ref[...]
    charge = jnp.zeros((1, atoms), jnp.float32)
    mass = jnp.zeros((1, atoms), jnp.float32)
    for kind in range(scale_ref.shape[1]):
        charge = jnp.where(species == kind, scale_ref[0:1, kind : kind + 1], charge)
        mass = jnp.where(species == kind, mass_ref[0:1, kind : kind + 1], mass)
    inverse = 1.0 / mass

    kick[...] = jnp.zeros(kick.shape, jnp.float32)
    if rows > 6 * per_device:
        state[0] = jnp.zeros((rows, atoms), jnp.float32)
    for component in range(3):
        at = row_of(component, 0, 0)
        state[0, at : at + per_device, :] = pos_ref[component]
        at = row_of(component, 1, 0)
        state[0, at : at + per_device, :] = mom_ref[component] * inverse

    def ghost_rows_of(block, side):
        chunks = [block[:, m * LANES : (m + 1) * LANES] for m in range(atom_chunks)]
        parts = []
        for g in range(ghost_chunks):
            index = ghost_ref[1 - side : 2 - side, g * LANES : (g + 1) * LANES]
            index = jnp.broadcast_to(index, (TILE, LANES))
            parts.append(pick(chunks, index & (LANES - 1), index // LANES))
        return parts

    def send_ghosts(step, extra):
        for side in range(2):
            for tile in range(rows // TILE + 1):
                at = tile * TILE
                block = extra if tile == rows // TILE else state[step, at : at + TILE, :]
                if block is None:
                    block = jnp.zeros((TILE, atoms), jnp.float32)
                for g, part in enumerate(ghost_rows_of(block, side)):
                    ghost_out[step, side, at : at + TILE, g * LANES : (g + 1) * LANES] = part
        return [
            to_side(ghost_out.at[step, side], ghost_in.at[step, side],
                    ghost_s.at[step], ghost_r.at[step], side)
            for side in range(2)
        ]

    def spread_row(row):
        return jnp.broadcast_to(row, (TILE, LANES))

    def ghost_window(buffer, lead, row):
        def parts(side):
            return [
                spread_row(buffer[(*lead, side, slice(row, row + 1), slice(g * LANES, (g + 1) * LANES))])
                for g in range(ghost_chunks)
            ]
        return parts(0), parts(1)

    def window_of(step, row):
        low, high = ghost_window(ghost_in, (step,), row)
        own = [
            spread_row(state[step, row : row + 1, m * LANES : (m + 1) * LANES])
            for m in range(atom_chunks)
        ]
        return low + own + high

    def cheap(step):
        @pl.loop(0, atom_chunks)
        def _(j):
            lanes = pl.ds(pl.multiple_of(j * LANES, LANES), LANES)
            factor = whole[1, 0:1, lanes]
            indices = [near_ref[k : k + TILE, lanes] for k in range(0, slots, TILE)]
            lows = [index & (LANES - 1) for index in indices]
            highs = [index // LANES for index in indices]
            for bead in range(per_device):
                offsets = []
                for component in range(3):
                    row = row_of(component, 0, bead)
                    chunks = window_of(step, row)
                    middle = spread_row(state[step, row : row + 1, lanes])
                    offsets.append(
                        [pick(chunks, low, high) - middle for low, high in zip(lows, highs)]
                    )
                totals = [None] * 3
                for t in range(len(indices)):
                    squared = sum(offsets[c][t] * offsets[c][t] for c in range(3))
                    strength = weight[t * TILE : (t + 1) * TILE, lanes] * jnp.exp(
                        -squared / pair_width
                    )
                    for c in range(3):
                        term = strength * offsets[c][t]
                        totals[c] = term if totals[c] is None else totals[c] + term
                for c in range(3):
                    row = row_of(c, 1, bead)
                    total = jnp.sum(totals[c], axis=0, keepdims=True)
                    kick[row : row + 1, lanes] = pair_strength * factor * total

    def learned(low_high, slot):
        rates = radial_rates(w_in_ref.shape[0])
        for t in range(cover // LANES):
            lanes = pl.ds(pl.multiple_of(first + t * LANES, LANES), LANES)
            indices = [near_ref[k : k + TILE, lanes] for k in range(0, slots, TILE)]
            offsets = []
            for c in range(3):
                low, high = low_high(c)
                own = [
                    spread_row(whole[0, c : c + 1, m * LANES : (m + 1) * LANES])
                    for m in range(atom_chunks)
                ]
                chunks = low + own + high
                middle = spread_row(whole[0, c : c + 1, lanes])
                offsets.append(
                    [pick(chunks, index & (LANES - 1), index // LANES) - middle for index in indices]
                )
            bases = []
            messages = [None] * len(rates)
            for k in range(len(indices)):
                squared = sum(offsets[c][k] * offsets[c][k] for c in range(3))
                basis = [jnp.exp(-float(rates[r]) * squared) for r in range(2)]
                for r in range(2, len(rates)):
                    basis.append(basis[r - 2] * basis[r - 2])
                bases.append(basis)
                strength = weight[k * TILE : (k + 1) * TILE, lanes]
                for r in range(len(rates)):
                    term = strength * basis[r]
                    messages[r] = term if messages[r] is None else messages[r] + term
            message = jnp.concatenate(
                [jnp.sum(m, axis=0, keepdims=True) for m in messages], axis=0
            ) / slots
            hidden = lax.dot_general(
                w_in_ref[...], message, (((0,), (0,)), ((), ())),
                precision=highest, preferred_element_type=jnp.float32,
            )
            hidden = hidden * jax.nn.sigmoid(hidden)
            radial = dot(w_out_ref[...], hidden)
            spread_radial = [spread_row(radial[r : r + 1, :]) for r in range(len(rates))]
            totals = [None] * 3
            for k in range(len(indices)):
                profile = sum(spread_radial[r] * bases[k][r] for r in range(len(rates)))
                strength = weight[k * TILE : (k + 1) * TILE, lanes] * profile
                for c in range(3):
                    term = strength * offsets[c][k]
                    totals[c] = term if totals[c] is None else totals[c] + term
            which = lax.broadcasted_iota(jnp.int32, (TILE, LANES), 0)
            tile = jnp.zeros((TILE, LANES), jnp.float32)
            for c in range(3):
                total = spread_row(jnp.sum(totals[c], axis=0, keepdims=True))
                tile = jnp.where(which == c, total, tile)
            piece[slot, me, :, t * LANES : (t + 1) * LANES] = tile

    def send_piece(slot):
        return [
            to_peer(piece.at[slot, me], piece.at[slot, me], piece_s.at[slot], piece_r.at[slot], j)
            for j in range(1, devices)
        ]

    def await_blocks(buffer, send, recv):
        for j in range(1, devices):
            to_peer(buffer.at[senders[j]], buffer.at[senders[j]], send, recv, j).wait_recv()

    def all_pieces(slot):
        parts = []
        for c in range(CB):
            line = []
            for m in range(atom_chunks):
                source = c * groups + m * LANES // share
                start = m * LANES - (source % groups) * share // LANES * LANES
                line.append(piece[slot, source, :, start : start + LANES])
            parts.append(jnp.concatenate(line, axis=1))
        return jnp.concatenate(parts, axis=0)

    sent = []

    def start(copies):
        for copy in copies:
            copy.start()
            sent.append(copy)

    parts = dot(table_ref[share_row : share_row + CB * TILE, 0:rows], state[0])
    for c in range(CB):
        part_out[c] = parts[c * TILE : (c + 1) * TILE, :]
    copies = [
        to_peer(part_out.at[peers[j] // groups], part_in.at[me], part_s, part_r, j)
        for j in range(1, devices)
    ]
    ghost_copies = send_ghosts(0, jnp.broadcast_to(charge, (TILE, atoms)))
    whole[1] = jnp.broadcast_to(charge * inverse, (TILE, atoms))

    pl.semaphore_wait(barrier, 3 * devices - 1)
    start(copies)
    start(ghost_copies)
    await_blocks(part_in, part_s, part_r)
    contracted = part_out[member]
    for j in range(1, devices):
        contracted = contracted + part_in[senders[j]]
    whole[0] = contracted
    for side in range(2):
        for g, part in enumerate(ghost_rows_of(contracted, side)):
            qghost_out[side, :, g * LANES : (g + 1) * LANES] = part
    qcopies = [
        to_side(qghost_out.at[side], qghost_in.at[side], qghost_s, qghost_r, side)
        for side in range(2)
    ]
    start(qcopies)
    for copy in ghost_copies:
        copy.wait_recv()

    low, high = ghost_window(ghost_in, (0,), rows)
    own = [spread_row(charge[:, m * LANES : (m + 1) * LANES]) for m in range(atom_chunks)]
    chunks = low + own + high
    for m in range(atom_chunks):
        lanes = slice(m * LANES, (m + 1) * LANES)
        itself = ghosts + m * LANES + lax.broadcasted_iota(jnp.int32, (TILE, LANES), 1)
        for k in range(0, slots, TILE):
            index = near_ref[k : k + TILE, lanes]
            value = pick(chunks, index & (LANES - 1), index // LANES)
            weight[k : k + TILE, lanes] = jnp.where(index == itself, 0.0, value)

    cheap(0)
    gathered[0, me] = state[0] + (0.5 * inner_step) * kick[...]
    start([
        to_peer(gathered.at[0, me], gathered.at[0, me], all_s.at[0], all_r.at[0], j)
        for j in range(1, devices)
    ])
    for copy in qcopies:
        copy.wait_recv()
    learned(lambda c: ghost_window(qghost_in, (), c), 0)
    start(send_piece(0))
    await_blocks(gathered.at[0], all_s.at[0], all_r.at[0])
    await_blocks(piece.at[0], piece_s.at[0], piece_r.at[0])

    for step in range(1, NINNER + 1):
        every = gathered[step - 1].reshape(devices * rows, atoms)
        extra = None
        if step == 1:
            every = jnp.concatenate((every, all_pieces(0) * inverse), axis=0)
            fresh = dot(table_ref[0:rows, :], every)
        elif step < NINNER:
            fresh = dot(table_ref[0:rows, 0:full], every)
        else:
            both = dot(table_ref[0 : moved_row + TILE, 0:full], every)
            fresh = both[0:rows]
            extra = both[moved_row:]
            whole[0] = extra
        state[step] = fresh
        if step == 1:
            ghost_copies = send_ghosts(step, extra)
            start(ghost_copies)
            for copy in ghost_copies:
                copy.wait_recv()
        else:
            await_edges(step - 2)
            for side in range(2):
                edge = edge_in[step - 2, side].reshape(full, ghosts)
                ghost_in[step, side] = dot(table_ref[0 : moved_row + TILE, 0:full], edge)
        if step == NINNER:
            learned(lambda c: ghost_window(ghost_in, (step,), rows + c), 1)
            start(send_piece(1))
        cheap(step)
        if step < NINNER:
            gathered[step, me] = state[step] + inner_step * kick[...]
            start([
                to_peer(gathered.at[step, me], gathered.at[step, me],
                        all_s.at[step], all_r.at[step], j)
                for j in range(1, devices)
            ])
            for side in range(2):
                for at in range(0, rows, TILE):
                    block = gathered[step, me, at : at + TILE, :]
                    for g, part in enumerate(ghost_rows_of(block, side)):
                        edge_out[step - 1, side, at : at + TILE, g * LANES : (g + 1) * LANES] = part
                start([to_edge(step - 1, side, j) for j in range(devices)])
            await_blocks(gathered.at[step], all_s.at[step], all_r.at[step])

    await_blocks(piece.at[1], piece_s.at[1], piece_r.at[1])
    kick[...] = (state[NINNER] + (0.5 * inner_step) * kick[...]) * mass + dot(
        table_ref[spread_row_at : spread_row_at + rows, 0 : CB * TILE], all_pieces(1)
    )
    for component in range(3):
        at = row_of(component, 0, 0)
        new_pos_ref[component] = state[NINNER, at : at + per_device, :]
        at = row_of(component, 1, 0)
        new_mom_ref[component] = kick[at : at + per_device, :]
    for copy in sent:
        copy.wait_send()


def body(
    positions, momenta, neighbours, ghost_rows, species, species_scale, mass_table, w_in, w_out
):
    per_device, _, atoms = positions.shape
    slots = neighbours.shape[0]
    ghosts = ghost_rows.shape[0] // 2
    devices = lax.axis_size("bead")
    table = tables(devices, per_device)
    rows = -(-6 * per_device // TILE) * TILE
    cover = max(atoms // (devices // CB), LANES)
    vmem = pl.BlockSpec(memory_space=pltpu.VMEM)
    hbm = pl.BlockSpec(memory_space=pltpu.HBM)
    f32 = jnp.float32
    dma = pltpu.SemaphoreType.DMA
    operands = (
        positions.transpose(1, 0, 2), momenta.transpose(1, 0, 2), neighbours,
        ghost_rows.reshape(2, ghosts), species.reshape(1, atoms), species_scale.reshape(1, -1),
        mass_table.reshape(1, -1), w_in.T, w_out, table,
    )
    shape = jax.ShapeDtypeStruct(operands[0].shape, f32)
    new_positions, new_momenta = pl.pallas_call(
        cycle_kernel,
        name="cycle",
        out_shape=(shape, shape),
        in_specs=[hbm] * 10,
        out_specs=(vmem, vmem),
        scratch_shapes=[
            pltpu.VMEM((NINNER + 1, rows, atoms), f32),
            pltpu.VMEM((rows, atoms), f32),
            pltpu.VMEM((slots, atoms), f32),
            pltpu.VMEM((NINNER, devices, rows, atoms), f32),
            pltpu.VMEM((NINNER + 1, 2, rows + TILE, ghosts), f32),
            pltpu.VMEM((NINNER + 1, 2, rows + TILE, ghosts), f32),
            pltpu.VMEM((CB, TILE, atoms), f32),
            pltpu.VMEM((devices, TILE, atoms), f32),
            pltpu.VMEM((2, TILE, atoms), f32),
            pltpu.VMEM((2, TILE, ghosts), f32),
            pltpu.VMEM((2, TILE, ghosts), f32),
            pltpu.VMEM((2, devices, TILE, cover), f32),
            pltpu.VMEM((NINNER - 1, 2, rows, ghosts), f32),
            pltpu.VMEM((NINNER - 1, 2, devices, rows, ghosts), f32),
            *[pltpu.VMEM(operand.shape, operand.dtype) for operand in operands[:-1]],
            pltpu.VMEM(table.shape[1:], f32),
            dma((len(operands),)),
            dma((NINNER - 1, 2, devices)), dma((NINNER - 1, 2, devices)),
            dma((devices,)), dma((devices,)),
            dma((NINNER + 1, 2)), dma((NINNER + 1, 2)),
            dma((2,)), dma((2,)),
            dma((NINNER, devices)), dma((NINNER, devices)),
            dma((2, devices)), dma((2, devices)),
        ],
        compiler_params=pltpu.CompilerParams(
            collective_id=0, has_side_effects=True, vmem_limit_bytes=67043328
        ),
    )(*operands)
    return (new_positions.transpose(1, 0, 2), new_momenta.transpose(1, 0, 2))


def solution(mesh):
    in_specs = (
        P("bead", None, "space"),
        P("bead", None, "space"),
        P(None, "space"),
        P("space"),
        P("space"),
        P(),
        P(),
        P(),
        P(),
    )
    out_specs = (P("bead", None, "space"), P("bead", None, "space"))
    return jax.shard_map(body, mesh=mesh, in_specs=in_specs, out_specs=out_specs, check_vma=False)
```

profile of v0, /device:TPU:0, one launch (start us, length us, event | category | flops | bytes accessed | tf_op | source)
XLA Modules:
  0.0 54.3 jit_solution(6794491219438597272)
XLA Ops:
  0.6 51.6 %cycle.1 = (f32[3,4,512]{2,1,0:T(4,128)}, f32[3,4,512]{2,1,0:T(4,128)}) custom-call(f32[3,4,512]{2,1,0:T(4,128)} %bitcast.9, f32[3,4,512]{2,1,0:T(4,128)} %bitcast.10, s32[32,512]{1,0:T(8,128)} %near_in.1, s32[2,128]{1,0:T(2,128)} %bitcast.15, s32[1,512]{1,0:T(1,128)} %bitcast.14, f32[1,2]{1,0:T(1,128)} %bitcast.16, f32[1,2]{1,0:T(1,128)} %bitcast.17, ...), custom_call_target="tpu_custom_call" | custom-call | tf_op jit(solution)/shard_map/cycle/pallas_call | solution.py:501
  52.3 0.0 copy-start
  52.3 1.4 %copy.14 = f32[4,3,512]{2,0,1:T(4,128)} copy(f32[4,3,512]{2,0,1:T(4,128)} %bitcast.12) | data formatting | bytes 49152
  53.7 0.0 copy-done
  53.7 0.6 %copy.15 = f32[4,3,512]{2,0,1:T(4,128)} copy(f32[4,3,512]{2,0,1:T(4,128)S(1)} %bitcast.11) | data formatting | bytes 49152
Async XLA Ops:
  52.3 1.4 %copy-start = (f32[3,4,512]{2,1,0:T(4,128)S(1)}, f32[3,4,512]{2,1,0:T(4,128)}, u32[]{:S(2)}) copy-start(f32[3,4,512]{2,1,0:T(4,128)} %get-tuple-element.5) | copy-start | bytes 73732
where the time goes:
time: 54.5 us; the launch traced here: 54.3 us
  Pallas kernels  51.6 us (95%)
  local copies, waits for them, and re-layouts  1.96 us (4%)
  between operations  0.65 us (1%)
    pallas_call x1, Pallas kernels, body(): pl.pallas_call(cycle_kernel, name='cycle', out_shape=(shape, shape), in_s...  51.6 us
    unnamed x4, local copies, waits for them, and re-layouts  1.96 us

commit v1 on v0

v1 whole, which is shorter than its diff:
```python
import jax
import jax.numpy as jnp
import numpy as np
from jax import lax
from jax.experimental import pallas as pl
from jax.experimental.pallas import tpu as pltpu
from jax.sharding import PartitionSpec as P

BEADS = 32
CB = 4
NINNER = 3


polymer_freq = 10.0
outer_step = 6.0
pair_width = 1.0
pair_strength = 1.0
highest = lax.Precision.HIGHEST


def mode_matrix(count):
    beadpos = np.arange(count)[None, :]
    modeidx = np.arange(count)[:, None]
    middle = count // 2
    cosine = np.sqrt(2.0 / count) * np.cos(2.0 * np.pi * beadpos * modeidx / count)
    sine_rows = np.sqrt(2.0 / count) * np.sin(2.0 * np.pi * beadpos * modeidx / count)
    matrix = np.where(modeidx < middle, cosine, sine_rows)
    matrix = np.where(modeidx == 0, 1.0 / np.sqrt(count), matrix)
    matrix = np.where(modeidx == middle, np.cos(np.pi * beadpos) / np.sqrt(count), matrix)
    return matrix


def mode_scales(count, inner_step):
    frequency = 2.0 * polymer_freq * np.sin(np.pi * np.arange(count) / count)
    nonzero = np.where(frequency > 0, frequency, 1.0)
    cosine = np.cos(frequency * inner_step)
    drift_gain = np.where(frequency > 0, np.sin(frequency * inner_step) / nonzero, inner_step)
    spring = frequency * np.sin(frequency * inner_step)
    return (cosine, drift_gain, spring)


def contraction(count, fewer):
    full_modes = mode_matrix(count)
    small_modes = mode_matrix(fewer)
    kept = list(range(fewer // 2 + 1)) + list(range(count - fewer // 2 + 1, count))
    contract = np.sqrt(fewer / count) * (small_modes.T @ full_modes[kept])
    expand = count / fewer * contract.T
    return (contract, expand)


def radial_rates(count):
    return 0.2 * 2.0 ** (np.arange(count) / 2.0)

LANES = 128
TILE = 8
KINDS = 5
MESH = pl.DeviceIdType.MESH


def layout(devices, per_device, atoms):
    groups_of = TILE // per_device
    halves = min(atoms // LANES, groups_of)
    return groups_of, halves, atoms // (halves * LANES)


def tables(devices, per_device, atoms):
    inner_step = outer_step / NINNER
    groups_of, halves, _ = layout(devices, per_device, atoms)
    modes = mode_matrix(BEADS)
    contract, expand = contraction(BEADS, CB)
    kick = 0.5 * outer_step * expand

    def power(count):
        cosine, drift_gain, spring = mode_scales(BEADS, inner_step)
        step = np.zeros((2 * BEADS, 2 * BEADS))
        step[:BEADS, :BEADS] = step[BEADS:, BEADS:] = modes.T @ (cosine[:, None] * modes)
        step[:BEADS, BEADS:] = modes.T @ (drift_gain[:, None] * modes)
        step[BEADS:, :BEADS] = -(modes.T @ (spring[:, None] * modes))
        whole = np.linalg.matrix_power(step, count)
        return (whole[:BEADS, :BEADS], whole[:BEADS, BEADS:], whole[BEADS:, :BEADS], whole[BEADS:, BEADS:])

    powers = [power(count) for count in range(NINNER + 1)]
    width = devices * TILE
    extra = halves * CB
    total = -(-(width + extra) // LANES) * LANES
    beads = np.arange(BEADS)
    column = beads // per_device * TILE + beads % per_device

    def block(matrix, device):
        out = np.zeros((TILE, width))
        for q in range(groups_of):
            for b in range(per_device):
                out[q * per_device + b, column + q * per_device] = matrix[device * per_device + b]
        return out

    def member_block(row):
        out = np.zeros((TILE, width))
        for q in range(groups_of):
            out[q, column + q * per_device] = row
        return out

    def piece_block(matrix, device):
        out = np.zeros((TILE, extra))
        for q in range(halves):
            for b in range(per_device):
                out[q * per_device + b, q * CB : (q + 1) * CB] = matrix[device * per_device + b]
        return out

    def piece_member_block(row):
        out = np.zeros((TILE, extra))
        for q in range(halves):
            out[q, q * CB : (q + 1) * CB] = row
        return out

    result = []
    for device in range(devices):
        chosen = contract[device // (devices // CB)]
        rows = []

        def add(left, right=None):
            line = np.zeros((left.shape[0], total))
            line[:, : left.shape[1]] = left
            if right is not None:
                line[:, width : width + extra] = right
            rows.append(line)

        share = np.zeros((CB * halves, TILE))
        for c in range(CB):
            for h in range(halves):
                for b in range(per_device):
                    share[c * halves + h, h * per_device + b] = contract[c, device * per_device + b]
        add(share)
        add(piece_block(kick, device))
        for count in range(1, NINNER + 1):
            add(block(powers[count][0], device))
        add(block(powers[NINNER][2], device))
        add(member_block(chosen @ powers[NINNER][0]))
        for start in range(NINNER):
            for count in range(1, NINNER + 1 - start):
                add(block(powers[count][1], device), piece_block(powers[count][1] @ kick, device))
            last = powers[NINNER - start]
            add(block(last[3], device), piece_block(last[3] @ kick, device))
            add(member_block(chosen @ last[1]), piece_member_block(chosen @ last[1] @ kick))
        result.append(np.concatenate(rows, axis=0))
    return jnp.asarray(np.stack(result), jnp.float32)


def dot(a, b):
    return jnp.dot(a, b, precision=highest, preferred_element_type=jnp.float32)


def lookup(chunk, low):
    return jnp.take_along_axis(chunk, low, axis=1, mode="promise_in_bounds")


def pick(chunks, low, high):
    found = None
    for number, chunk in enumerate(chunks):
        value = lookup(chunk, low)
        found = value if found is None else jnp.where(high == number, value, found)
    return found


def cycle_kernel(
    pos_in, mom_in, near_in, ghost_from, species_in, scale_in, mass_in, w_in_in, w_out_in, table_in,
    new_pos_ref, new_mom_ref,
    first_pos, first_vel, inv_ref, factor_ref, mass_rows, weight, kick, acc, ghost_acc,
    begin, kicks, zg_out, zg_in, part_line, part_out, part_in, q_own, qg_out, qg_in, piece,
    free_out, free_in, edge_out, edge_in,
    pos_ref, mom_ref, near_ref, ghost_ref, species_ref, scale_ref, mass_ref, w_in_ref, w_out_ref,
    table_ref, load_s, zg_s, zg_r, part_s, part_r, begin_s, begin_r, qg_s, qg_r, kick_s, kick_r,
    piece_s, piece_r, free_s, free_r, edge_s, edge_r,
):
    _, per_device, atoms = pos_ref.shape
    slots = near_ref.shape[0]
    ghosts = ghost_ref.shape[1]
    devices = lax.axis_size("bead")
    domains = lax.axis_size("space")
    me = lax.axis_index("bead")
    domain = lax.axis_index("space")
    above = lax.rem(domain + 1, domains)
    below = lax.rem(domain + domains - 1, domains)
    inner_step = outer_step / NINNER
    groups_of, halves, strips = layout(devices, per_device, atoms)
    wide = 3 * LANES
    used = halves * per_device
    ghost_tiles = -(-3 // groups_of)
    groups = devices // CB
    share = atoms // groups
    cover = max(share, LANES)
    member = me // groups
    first = lax.rem(me, groups) * share // LANES * LANES
    atom_chunks = atoms // LANES
    width = devices * TILE
    extra = halves * CB

    def partner(j):
        at, bit = me, 1
        while bit < devices:
            if j & bit:
                at = at + bit - 2 * bit * lax.rem(at // bit, 2)
            bit *= 2
        return at

    peers = [partner(j) for j in range(devices)]
    order = list(range(devices - 1, 0, -1))

    pairs = (
        (pos_in, pos_ref), (mom_in, mom_ref), (species_in, species_ref), (scale_in, scale_ref),
        (mass_in, mass_ref), (ghost_from, ghost_ref), (table_in.at[me], table_ref),
        (near_in, near_ref), (w_in_in, w_in_ref), (w_out_in, w_out_ref),
    )
    loads = [
        pltpu.make_async_copy(src, dst, load_s.at[number])
        for number, (src, dst) in enumerate(pairs)
    ]
    for load in loads:
        load.start()
    barrier = pltpu.get_barrier_semaphore()
    for j in order:
        pl.semaphore_signal(barrier, inc=1, device_id={"bead": peers[j]}, device_id_type=MESH)
    for target in (above, below):
        pl.semaphore_signal(barrier, inc=1, device_id={"space": target}, device_id_type=MESH)

    def to_peer(src, dst, send, recv, j):
        return pltpu.make_async_remote_copy(
            src_ref=src, dst_ref=dst, send_sem=send.at[j], recv_sem=recv.at[j],
            device_id={"bead": peers[j]}, device_id_type=MESH,
        )

    def to_side(src, dst, send, recv, side):
        return pltpu.make_async_remote_copy(
            src_ref=src, dst_ref=dst, send_sem=send.at[side], recv_sem=recv.at[side],
            device_id={"space": (above, below)[side]}, device_id_type=MESH,
        )

    def to_edge(step, side, j, sender):
        return pltpu.make_async_remote_copy(
            src_ref=edge_out.at[step, side], dst_ref=edge_in.at[step, side, sender],
            send_sem=edge_s.at[step, side, j], recv_sem=edge_r.at[step, side, j],
            device_id={"bead": peers[j], "space": (above, below)[side]}, device_id_type=MESH,
        )

    sent = []

    def start(copies):
        for copy in copies:
            copy.start()
            sent.append(copy)

    def await_blocks(buffer, send, recv):
        for j in order:
            to_peer(buffer.at[peers[j]], buffer.at[peers[j]], send, recv, j).wait_recv()

    row_at = lax.broadcasted_iota(jnp.int32, (TILE, LANES), 0)

    def spread_row(row):
        return jnp.broadcast_to(row, (TILE, LANES))

    def lane_of(strip, c):
        at = (strip * 3 + c) * LANES
        return slice(at, at + LANES)

    def chunk_of(m):
        return slice(m * LANES, (m + 1) * LANES)

    def fold(value, unit):
        shift = unit
        while shift < TILE:
            value = value + pltpu.roll(value, shift, 0)
            shift *= 2
        return value

    def index_of(side):
        index = spread_row(ghost_ref[1 - side : 2 - side, :])
        return index & (LANES - 1), index // LANES

    def ghost_values(ref, lead, side, unit):
        low, high = index_of(side)
        half = high // strips
        strip_at = high - half * strips
        values = []
        for c in range(3):
            parts = [lookup(ref[(*lead, slice(None), lane_of(s, c))], low) for s in range(strips)]
            value = parts[0]
            for s in range(1, strips):
                value = jnp.where(strip_at == s, parts[s], value)
            value = jnp.where(row_at // unit == half, value, 0.0)
            values.append(fold(value, unit))
        return values

    def compose(values, unit):
        tiles = []
        for t in range(ghost_tiles):
            tile = jnp.zeros((TILE, LANES), jnp.float32)
            for c in range(t * groups_of, min(len(values), (t + 1) * groups_of)):
                tile = jnp.where(row_at // unit == c % groups_of, values[c], tile)
            tiles.append(tile)
        return tiles

    for load in loads[:7]:
        load.wait()
    species = species_ref[...]
    charge = jnp.zeros((1, atoms), jnp.float32)
    mass = jnp.zeros((1, atoms), jnp.float32)
    for kind in range(scale_ref.shape[1]):
        charge = jnp.where(species == kind, scale_ref[0:1, kind : kind + 1], charge)
        mass = jnp.where(species == kind, mass_ref[0:1, kind : kind + 1], mass)
    inverse = 1.0 / mass
    factor_ref[...] = charge * inverse

    if used < TILE:
        first_pos[...] = jnp.zeros(first_pos.shape, jnp.float32)
        first_vel[...] = jnp.zeros(first_vel.shape, jnp.float32)
        kick[...] = jnp.zeros(kick.shape, jnp.float32)
        inv_ref[...] = jnp.zeros(inv_ref.shape, jnp.float32)
        mass_rows[...] = jnp.zeros(mass_rows.shape, jnp.float32)
    for h in range(halves):
        at = slice(h * per_device, (h + 1) * per_device)
        for s in range(strips):
            chunk = chunk_of(h * strips + s)
            for c in range(3):
                first_pos[at, lane_of(s, c)] = pos_ref[c, :, chunk]
    begin[me] = first_pos[...]
    charge_ghosts = []
    for side in range(2):
        low, high = index_of(side)
        parts = [spread_row(charge[:, chunk_of(m)]) for m in range(atom_chunks)]
        values = ghost_values(first_pos, (), side, per_device) + [pick(parts, low, high)]
        for t, tile in enumerate(compose(values, per_device)):
            zg_out[0, side, t * TILE : (t + 1) * TILE, :] = tile

    part_line[0:extra, :] = dot(table_ref[0:extra, 0:TILE], first_pos[...])
    for c in range(CB):
        for i in range(3):
            for m in range(atom_chunks):
                h, s = m // strips, m % strips
                row = c * halves + h
                at = i * atom_chunks + m
                part_out[c, at : at + 1, :] = part_line[row : row + 1, lane_of(s, i)]

    pl.semaphore_wait(barrier, devices + 1)
    ghost_copies = [
        to_side(zg_out.at[0, side], zg_in.at[0, side], zg_s.at[0], zg_r.at[0], side)
        for side in range(2)
    ]
    start(ghost_copies)
    start([to_peer(part_out.at[peers[j] // groups], part_in.at[me], part_s, part_r, j) for j in order])
    start([to_peer(begin.at[me], begin.at[me], begin_s, begin_r, j) for j in order])

    for h in range(halves):
        at = slice(h * per_device, (h + 1) * per_device)
        for s in range(strips):
            chunk = chunk_of(h * strips + s)
            own = jnp.broadcast_to(inverse[:, chunk], (per_device, LANES))
            inv_ref[at, chunk_of(s)] = own
            mass_rows[at, chunk_of(s)] = jnp.broadcast_to(mass[:, chunk], (per_device, LANES))
            for c in range(3):
                first_vel[at, lane_of(s, c)] = mom_ref[c, :, chunk] * own

    await_blocks(part_in, part_s, part_r)
    contracted = part_out[member]
    for j in order:
        contracted = contracted + part_in[peers[j]]
    part_line[0 : contracted.shape[0], 0:LANES] = contracted

    def put_q(value_of):
        for i in range(3):
            for m in range(atom_chunks):
                q_own[i : i + 1, chunk_of(m)] = value_of(i, m)

    put_q(lambda i, m: part_line[i * atom_chunks + m : i * atom_chunks + m + 1, 0:LANES])
    for side in range(2):
        low, high = index_of(side)
        qg_out[side] = pick([q_own[:, chunk_of(m)] for m in range(atom_chunks)], low, high)
    qcopies = [to_side(qg_out.at[side], qg_in.at[side], qg_s, qg_r, side) for side in range(2)]
    start(qcopies)
    for load in loads[7:]:
        load.wait()
    for copy in ghost_copies:
        copy.wait_recv()

    def ghost_row(ref, lead, side, c, b):
        at = c // groups_of * TILE + c % groups_of * per_device + b
        return spread_row(ref[(*lead, side, slice(at, at + 1), slice(None))])

    chunks = [ghost_row(zg_in, (0,), 0, 3, 0)]
    chunks += [spread_row(charge[:, chunk_of(m)]) for m in range(atom_chunks)]
    chunks += [ghost_row(zg_in, (0,), 1, 3, 0)]
    for m in range(atom_chunks):
        itself = ghosts + m * LANES + lax.broadcasted_iota(jnp.int32, (TILE, LANES), 1)
        for k in range(0, slots, TILE):
            index = near_ref[k : k + TILE, chunk_of(m)]
            value = pick(chunks, index & (LANES - 1), index // LANES)
            weight[k : k + TILE, chunk_of(m)] = jnp.where(index == itself, 0.0, value)

    def cheap(own_ref, own_lead, ghost_ref_of, ghost_lead, finish):
        for s in range(strips):
            for h in range(halves):
                lanes = chunk_of(h * strips + s)
                factor = factor_ref[:, lanes]
                indices = [near_ref[k : k + TILE, lanes] for k in range(0, slots, TILE)]
                lows = [index & (LANES - 1) for index in indices]
                highs = [index // LANES for index in indices]
                for b in range(per_device):
                    offsets = []
                    for c in range(3):
                        def own_row(m):
                            at = m // strips * per_device + b
                            return spread_row(
                                own_ref[(*own_lead, slice(at, at + 1), lane_of(m % strips, c))]
                            )
                        sources = [ghost_row(ghost_ref_of, ghost_lead, 0, c, b)]
                        sources += [own_row(m) for m in range(atom_chunks)]
                        sources += [ghost_row(ghost_ref_of, ghost_lead, 1, c, b)]
                        middle = own_row(h * strips + s)
                        offsets.append(
                            [pick(sources, low, high) - middle for low, high in zip(lows, highs)]
                        )
                    totals = [None] * 3
                    for t in range(len(indices)):
                        squared = sum(offsets[c][t] * offsets[c][t] for c in range(3))
                        strength = weight[t * TILE : (t + 1) * TILE, lanes] * jnp.exp(
                            -squared / pair_width
                        )
                        for c in range(3):
                            term = strength * offsets[c][t]
                            totals[c] = term if totals[c] is None else totals[c] + term
                    at = h * per_device + b
                    for c in range(3):
                        total = jnp.sum(totals[c], axis=0, keepdims=True)
                        kick[at : at + 1, lane_of(s, c)] = pair_strength * factor * total
            finish(s)

    def learned(low_high, slot):
        rates = radial_rates(w_in_ref.shape[0])
        for t in range(cover // LANES):
            lanes = pl.ds(pl.multiple_of(first + t * LANES, LANES), LANES)
            indices = [near_ref[k : k + TILE, lanes] for k in range(0, slots, TILE)]
            offsets = []
            for c in range(3):
                low, high = low_high(c)
                own = [spread_row(q_own[c : c + 1, chunk_of(m)]) for m in range(atom_chunks)]
                chunks = [low] + own + [high]
                middle = spread_row(q_own[c : c + 1, lanes])
                offsets.append(
                    [pick(chunks, index & (LANES - 1), index // LANES) - middle for index in indices]
                )
            bases = []
            messages = [None] * len(rates)
            for k in range(len(indices)):
                squared = sum(offsets[c][k] * offsets[c][k] for c in range(3))
                basis = [jnp.exp(-float(rates[r]) * squared) for r in range(2)]
                for r in range(2, len(rates)):
                    basis.append(basis[r - 2] * basis[r - 2])
                bases.append(basis)
                strength = weight[k * TILE : (k + 1) * TILE, lanes]
                for r in range(len(rates)):
                    term = strength * basis[r]
                    messages[r] = term if messages[r] is None else messages[r] + term
            message = jnp.concatenate(
                [jnp.sum(m, axis=0, keepdims=True) for m in messages], axis=0
            ) / slots
            hidden = lax.dot_general(
                w_in_ref[...], message, (((0,), (0,)), ((), ())),
                precision=highest, preferred_element_type=jnp.float32,
            )
            hidden = hidden * jax.nn.sigmoid(hidden)
            radial = dot(w_out_ref[...], hidden)
            spread_radial = [spread_row(radial[r : r + 1, :]) for r in range(len(rates))]
            totals = [None] * 3
            for k in range(len(indices)):
                profile = sum(spread_radial[r] * bases[k][r] for r in range(len(rates)))
                strength = weight[k * TILE : (k + 1) * TILE, lanes] * profile
                for c in range(3):
                    term = strength * offsets[c][k]
                    totals[c] = term if totals[c] is None else totals[c] + term
            tile = jnp.zeros((TILE, LANES), jnp.float32)
            for c in range(3):
                total = spread_row(jnp.sum(totals[c], axis=0, keepdims=True))
                tile = jnp.where(row_at % 4 == c, total, tile)
            tile = jnp.where(row_at // 4 == t % 2, tile, 0.0)
            at = t // 2 * TILE
            if t % 2:
                tile = tile + piece[slot, me, at : at + TILE, :]
            piece[slot, me, at : at + TILE, :] = tile
        start([
            to_peer(piece.at[slot, me], piece.at[slot, me], piece_s.at[slot], piece_r.at[slot], j)
            for j in order
        ])

    def all_pieces(slot, scale):
        line = []
        for s in range(strips):
            for i in range(3):
                tiles = []
                for top in range(0, extra, TILE):
                    tile = jnp.zeros((TILE, LANES), jnp.float32)
                    for row in range(top, min(extra, top + TILE)):
                        h, c = row // CB, row % CB
                        m = h * strips + s
                        source = c * groups + m * LANES // share
                        t = (m * LANES - (source % groups) * share // LANES * LANES) // LANES
                        at = t // 2 * TILE + t % 2 * 4 + i
                        value = piece[slot, source, at : at + 1, :]
                        if scale is not None:
                            value = value * scale[:, chunk_of(m)]
                        tile = jnp.where(row_at == row - top, spread_row(value), tile)
                    tiles.append(tile)
                line.append(jnp.concatenate(tiles, axis=0))
        return jnp.concatenate(line, axis=1)

    def send_kick(step):
        def finish(s):
            lanes = slice(s * wide, (s + 1) * wide)
            if step == 0:
                kicks[0, me, :, lanes] = first_vel[:, lanes] + (0.5 * inner_step) * kick[:, lanes]
            else:
                kick[:, lanes] = inner_step * kick[:, lanes]
                kicks[step, me, :, lanes] = kick[:, lanes]
            start([
                to_peer(kicks.at[step, me, :, lanes], kicks.at[step, me, :, lanes],
                        kick_s.at[step, s], kick_r.at[step, s], j)
                for j in order
            ])
        return finish

    def await_kick(step):
        for s in range(strips):
            lanes = slice(s * wide, (s + 1) * wide)
            for j in order:
                block = kicks.at[step, peers[j], :, lanes]
                to_peer(block, block, kick_s.at[step, s], kick_r.at[step, s], j).wait_recv()

    base_row = extra + TILE
    step_row = [base_row + KINDS * TILE]
    for step in range(NINNER):
        step_row.append(step_row[-1] + (KINDS - step) * TILE)

    cheap(first_pos, (), zg_in, (0,), send_kick(0))
    await_blocks(begin, begin_s, begin_r)
    based = dot(table_ref[base_row : base_row + KINDS * TILE, 0:width], begin[...].reshape(width, -1))
    for copy in qcopies:
        copy.wait_recv()
    learned(lambda c: [spread_row(qg_in[side, c : c + 1, :]) for side in range(2)], 0)
    await_kick(0)
    await_blocks(piece.at[0], piece_s.at[0], piece_r.at[0])
    every = jnp.concatenate((kicks[0].reshape(width, -1), all_pieces(0, inverse)), axis=0)
    based = based + dot(table_ref[step_row[0] : step_row[1], 0 : width + extra], every)
    for kind in range(KINDS):
        acc[kind] = based[kind * TILE : (kind + 1) * TILE, :]

    for side in range(2):
        for t, tile in enumerate(compose(ghost_values(acc, (0,), side, per_device), per_device)):
            zg_out[1, side, t * TILE : (t + 1) * TILE, :] = tile
    ghost_copies = [
        to_side(zg_out.at[1, side], zg_in.at[1, side], zg_s.at[1], zg_r.at[1], side)
        for side in range(2)
    ]
    start(ghost_copies)
    for side in range(2):
        for number, (kind, unit) in enumerate(((1, per_device), (2, per_device), (4, 1))):
            for t, tile in enumerate(compose(ghost_values(acc, (kind,), side, unit), unit)):
                at = (number * ghost_tiles + t) * TILE
                free_out[side, at : at + TILE, :] = tile
    free_copies = [
        to_side(free_out.at[side], free_in.at[side], free_s, free_r, side) for side in range(2)
    ]
    start(free_copies)
    for copy in ghost_copies:
        copy.wait_recv()

    def send_edges(step):
        for side in range(2):
            tiles = compose(ghost_values(kick, (), side, per_device), per_device)
            for t, tile in enumerate(tiles):
                rows = min(TILE, 3 * per_device - t * TILE)
                edge_out[step - 1, side, t * TILE : t * TILE + rows, :] = tile[0:rows]
        start([to_edge(step - 1, side, j, me) for j in order + [0] for side in range(2)])

    def await_edges(step):
        for j in order + [0]:
            for side in range(2):
                to_edge(step - 1, side, j, peers[j]).wait_recv()
        lines = []
        for side in range(2):
            for t in range(ghost_tiles):
                rows = min(TILE, 3 * per_device - t * TILE)
                tiles = []
                for device in range(devices):
                    tile = edge_in[step - 1, side, device, t * TILE : t * TILE + rows, :]
                    if rows < TILE:
                        tile = jnp.concatenate(
                            (tile, jnp.zeros((TILE - rows, LANES), jnp.float32)), axis=0
                        )
                    tiles.append(tile)
                lines.append(jnp.concatenate(tiles, axis=0))
        return jnp.concatenate(lines, axis=1)

    cheap(acc, (0,), zg_in, (1,), send_kick(1))
    send_edges(1)
    for copy in free_copies:
        copy.wait_recv()
    for step in range(1, NINNER):
        await_kick(step)
        table = table_ref[step_row[step] : step_row[step + 1], 0:width]
        moved = dot(table, kicks[step].reshape(width, -1))
        for kind in range(step, KINDS):
            at = (kind - step) * TILE
            acc[kind] = acc[kind] + moved[at : at + TILE, :]
        moved = dot(table, await_edges(step))
        for side in range(2):
            for number, kind in enumerate((1, 2, 4)):
                if kind < step:
                    continue
                at = (kind - step) * TILE
                for t in range(ghost_tiles):
                    line = (side * ghost_tiles + t) * LANES
                    held = (number * ghost_tiles + t) * TILE
                    old = free_in if step == 1 else ghost_acc
                    ghost_acc[side, held : held + TILE, :] = (
                        old[side, held : held + TILE, :] + moved[at : at + TILE, line : line + LANES]
                    )
        if step + 1 == NINNER:
            put_q(lambda i, m: acc[4, m // strips : m // strips + 1, lane_of(m % strips, i)])

            def low_high(c):
                at = (2 * ghost_tiles + c // groups_of) * TILE + c % groups_of
                return [spread_row(ghost_acc[side, at : at + 1, :]) for side in range(2)]

            learned(low_high, 1)
        shifted = ghost_acc.at[:, step_tile(step, ghost_tiles), :]
        if step + 1 < NINNER:
            cheap(acc, (step,), shifted, (), send_kick(step + 1))
            send_edges(step + 1)
        else:
            cheap(acc, (step,), shifted, (), lambda s: None)

    for h in range(halves):
        at = slice(h * per_device, (h + 1) * per_device)
        for s in range(strips):
            for c in range(3):
                new_pos_ref[c, :, chunk_of(h * strips + s)] = acc[2, at, lane_of(s, c)]
    await_blocks(piece.at[1], piece_s.at[1], piece_r.at[1])
    slow = dot(table_ref[extra : extra + TILE, 0:extra], all_pieces(1, None))
    for s in range(strips):
        heavy = mass_rows[:, chunk_of(s)]
        for c in range(3):
            lanes = lane_of(s, c)
            kick[:, lanes] = (
                acc[3, :, lanes] + (0.5 * inner_step) * kick[:, lanes]
            ) * heavy + slow[:, lanes]
    for h in range(halves):
        at = slice(h * per_device, (h + 1) * per_device)
        for s in range(strips):
            for c in range(3):
                new_mom_ref[c, :, chunk_of(h * strips + s)] = kick[at, lane_of(s, c)]
    for copy in sent:
        copy.wait_send()


def step_tile(step, ghost_tiles):
    return slice((step - 1) * ghost_tiles * TILE, step * ghost_tiles * TILE)


def body(
    positions, momenta, neighbours, ghost_rows, species, species_scale, mass_table, w_in, w_out
):
    per_device, _, atoms = positions.shape
    slots = neighbours.shape[0]
    ghosts = ghost_rows.shape[0] // 2
    devices = lax.axis_size("bead")
    table = tables(devices, per_device, atoms)
    groups_of, halves, strips = layout(devices, per_device, atoms)
    ghost_tiles = -(-3 // groups_of)
    extra = halves * CB
    lanes = 3 * LANES * strips
    cover = max(atoms // (devices // CB), LANES)
    lines = -(-3 * (atoms // LANES) // TILE) * TILE
    piece_rows = -(-(cover // LANES) // 2) * TILE
    vmem = pl.BlockSpec(memory_space=pltpu.VMEM)
    hbm = pl.BlockSpec(memory_space=pltpu.HBM)
    f32 = jnp.float32
    dma = pltpu.SemaphoreType.DMA
    operands = (
        positions.transpose(1, 0, 2), momenta.transpose(1, 0, 2), neighbours,
        ghost_rows.reshape(2, ghosts), species.reshape(1, atoms), species_scale.reshape(1, -1),
        mass_table.reshape(1, -1), w_in.T, w_out, table,
    )
    shape = jax.ShapeDtypeStruct(operands[0].shape, f32)
    new_positions, new_momenta = pl.pallas_call(
        cycle_kernel,
        name="cycle",
        out_shape=(shape, shape),
        in_specs=[hbm] * 10,
        out_specs=(vmem, vmem),
        scratch_shapes=[
            pltpu.VMEM((TILE, lanes), f32),
            pltpu.VMEM((TILE, lanes), f32),
            pltpu.VMEM((TILE, strips * LANES), f32),
            pltpu.VMEM((1, atoms), f32),
            pltpu.VMEM((TILE, strips * LANES), f32),
            pltpu.VMEM((slots, atoms), f32),
            pltpu.VMEM((TILE, lanes), f32),
            pltpu.VMEM((KINDS, TILE, lanes), f32),
            pltpu.VMEM((2, 3 * ghost_tiles * TILE, ghosts), f32),
            pltpu.VMEM((devices, TILE, lanes), f32),
            pltpu.VMEM((NINNER, devices, TILE, lanes), f32),
            pltpu.VMEM((2, 2, ghost_tiles * TILE, ghosts), f32),
            pltpu.VMEM((2, 2, ghost_tiles * TILE, ghosts), f32),
            pltpu.VMEM((max(extra, lines), lanes), f32),
            pltpu.VMEM((CB, lines, LANES), f32),
            pltpu.VMEM((devices, lines, LANES), f32),
            pltpu.VMEM((TILE, atoms), f32),
            pltpu.VMEM((2, TILE, ghosts), f32),
            pltpu.VMEM((2, TILE, ghosts), f32),
            pltpu.VMEM((2, devices, piece_rows, LANES), f32),
            pltpu.VMEM((2, 3 * ghost_tiles * TILE, ghosts), f32),
            pltpu.VMEM((2, 3 * ghost_tiles * TILE, ghosts), f32),
            pltpu.VMEM((NINNER - 1, 2, 3 * per_device, ghosts), f32),
            pltpu.VMEM((NINNER - 1, 2, devices, 3 * per_device, ghosts), f32),
            *[pltpu.VMEM(operand.shape, operand.dtype) for operand in operands[:-1]],
            pltpu.VMEM(table.shape[1:], f32),
            dma((len(operands),)),
            dma((2, 2)), dma((2, 2)),
            dma((devices,)), dma((devices,)),
            dma((devices,)), dma((devices,)),
            dma((2,)), dma((2,)),
            dma((NINNER, strips, devices)), dma((NINNER, strips, devices)),
            dma((2, devices)), dma((2, devices)),
            dma((2,)), dma((2,)),
            dma((NINNER - 1, 2, devices)), dma((NINNER - 1, 2, devices)),
        ],
        compiler_params=pltpu.CompilerParams(
            collective_id=0, has_side_effects=True, vmem_limit_bytes=16777216
        ),
    )(*operands)
    return (new_positions.transpose(1, 0, 2), new_momenta.transpose(1, 0, 2))


def solution(mesh):
    in_specs = (
        P("bead", None, "space"),
        P("bead", None, "space"),
        P(None, "space"),
        P("space"),
        P("space"),
        P(),
        P(),
        P(),
        P(),
    )
    out_specs = (P("bead", None, "space"), P("bead", None, "space"))
    return jax.shard_map(body, mesh=mesh, in_specs=in_specs, out_specs=out_specs, check_vma=False)
```

time: 54.5 us -> 48.7 us (0.89)
  Pallas kernels: 51.6 us -> 42.3 us
  local copies, waits for them, and re-layouts: 1.96 us -> 5.31 us
    pallas_call x1, Pallas kernels: 51.6 us -> 42.3 us  [body(): pl.pallas_call(cycle_kernel, name='cycle', out_shape=(shape, shape), in_s...]
    unnamed x4 -> x22, local copies, waits for them, and re-layouts: 1.96 us -> 5.31 us
where the time goes in v1:
time: 48.7 us; the launch traced here: 48.3 us
  Pallas kernels  42.3 us (87%)
  local copies, waits for them, and re-layouts  5.31 us (11%)
  between operations  0.7 us (1%)
    pallas_call x1, Pallas kernels, body(): pl.pallas_call(cycle_kernel, name='cycle', out_shape=(shape, shape), in_s...  42.3 us
    unnamed x22, local copies, waits for them, and re-layouts  5.31 us

profile of v1, /device:TPU:0, one launch (start us, length us, event | category | flops | bytes accessed | tf_op | source)
XLA Modules:
  0.0 48.3 jit_solution(2471562673061209048)
XLA Ops:
  0.6 0.0 copy-start.8
  0.6 0.0 copy-start.9
  0.7 0.0 copy-start.6
  0.7 0.0 copy-start.5
  0.7 0.0 copy-start.4
  0.7 0.0 copy-start.7
  0.7 0.6 %copy-done.8 = f32[2]{0:T(128)S(1)} copy-done((f32[2]{0:T(128)S(1)}, f32[2]{0:T(128)}, u32[]{:S(2)}) %copy-start.8) | copy-done | bytes 32
  1.3 0.0 copy-done.9
  1.3 0.0 copy-done.6
  1.3 0.0 copy-done.5
  1.4 0.0 copy-done.4
  1.4 0.0 copy-done.7
  1.4 0.0 copy-start
  1.4 1.1 %copy-done = f32[8,152,128]{2,1,0:T(8,128)S(1)} copy-done((f32[8,152,128]{2,1,0:T(8,128)S(1)}, f32[8,152,128]{2,1,0:T(8,128)}, u32[]{:S(2)}) %copy-start) | copy-done | bytes 622616
  2.5 0.0 copy-start.1
  2.5 0.8 %copy-done.1 = s32[32,512]{1,0:T(8,128)S(1)} copy-done((s32[32,512]{1,0:T(8,128)S(1)}, s32[32,512]{1,0:T(8,128)}, u32[]{:S(2)}) %copy-start.1) | copy-done | bytes 65560
  3.3 0.0 copy-start.2
  3.3 0.7 %copy-done.2 = f32[4,3,512]{2,0,1:T(4,128)S(1)} copy-done((f32[4,3,512]{2,0,1:T(4,128)S(1)}, f32[4,3,512]{2,0,1:T(4,128)}, u32[]{:S(2)}) %copy-start.2) | copy-done | bytes 24600
  4.0 0.0 copy-start.3
  4.0 0.7 %copy-done.3 = f32[4,3,512]{2,0,1:T(4,128)S(1)} copy-done((f32[4,3,512]{2,0,1:T(4,128)S(1)}, f32[4,3,512]{2,0,1:T(4,128)}, u32[]{:S(2)}) %copy-start.3) | copy-done | bytes 24600
  4.8 42.3 %cycle.1 = (f32[3,4,512]{2,1,0:T(4,128)S(1)}, f32[3,4,512]{2,1,0:T(4,128)S(1)}) custom-call(f32[3,4,512]{2,1,0:T(4,128)S(1)} %bitcast.9, f32[3,4,512]{2,1,0:T(4,128)S(1)} %bitcast.10, s32[32,512]{1,0:T(8,128)S(1)} %copy-done.1, s32[2,128]{1,0:T(2,128)S(1)} %bitcast.15, s32[1,512]{1,0:T(1,128)S(1)} %bitcast.14, f32[1,2]{1,0:T(1,128)S(1)} %bitcast.16, ...), custom_call_target="tpu_custom_call" | custom-call | tf_op jit(solution)/shard_map/cycle/pallas_call | solution.py:691
  47.1 0.6 %copy.14 = f32[4,3,512]{2,0,1:T(4,128)} copy(f32[4,3,512]{2,0,1:T(4,128)S(1)} %bitcast.12) | data formatting | bytes 49152
  47.7 0.6 %copy.15 = f32[4,3,512]{2,0,1:T(4,128)} copy(f32[4,3,512]{2,0,1:T(4,128)S(1)} %bitcast.11) | data formatting | bytes 49152
Async XLA Ops:
  0.6 0.7 %copy-start.8 = (f32[2]{0:T(128)S(1)}, f32[2]{0:T(128)}, u32[]{:S(2)}) copy-start(f32[2]{0:T(128)} %param.15) | copy-start | bytes 28
  0.6 0.7 %copy-start.9 = (f32[2]{0:T(128)S(1)}, f32[2]{0:T(128)}, u32[]{:S(2)}) copy-start(f32[2]{0:T(128)} %param.16) | copy-start | bytes 28
  0.7 0.7 %copy-start.6 = (s32[512]{0:T(512)S(1)}, s32[512]{0:T(512)}, u32[]{:S(2)}) copy-start(s32[512]{0:T(512)} %param.14) | copy-start | bytes 6148
  0.7 0.7 %copy-start.5 = (f32[8,128]{1,0:T(8,128)S(1)}, f32[8,128]{1,0:T(8,128)}, u32[]{:S(2)}) copy-start(f32[8,128]{1,0:T(8,128)} %w_out_in.1) | copy-start | bytes 12292
  0.7 0.7 %copy-start.4 = (f32[128,8]{0,1:T(8,128)S(1)}, f32[128,8]{0,1:T(8,128)}, u32[]{:S(2)}) copy-start(f32[128,8]{0,1:T(8,128)} %param.17) | copy-start | bytes 12292
  0.7 0.7 %copy-start.7 = (s32[256]{0:T(256)S(1)}, s32[256]{0:T(256)}, u32[]{:S(2)}) copy-start(s32[256]{0:T(256)} %param.13) | copy-start | bytes 3076
  1.4 1.1 %copy-start = (f32[8,152,128]{2,1,0:T(8,128)S(1)}, f32[8,152,128]{2,1,0:T(8,128)}, u32[]{:S(2)}) copy-start(f32[8,152,128]{2,1,0:T(8,128)} %constant.2.clone.table_in) | copy-start | bytes 1867780
  2.5 0.8 %copy-start.1 = (s32[32,512]{1,0:T(8,128)S(1)}, s32[32,512]{1,0:T(8,128)}, u32[]{:S(2)}) copy-start(s32[32,512]{1,0:T(8,128)} %near_in.1) | copy-start | bytes 196612
  3.3 0.7 %copy-start.2 = (f32[4,3,512]{2,0,1:T(4,128)S(1)}, f32[4,3,512]{2,0,1:T(4,128)}, u32[]{:S(2)}) copy-start(f32[4,3,512]{2,0,1:T(4,128)} %param.10) | copy-start | bytes 73732
  4.0 0.7 %copy-start.3 = (f32[4,3,512]{2,0,1:T(4,128)S(1)}, f32[4,3,512]{2,0,1:T(4,128)}, u32[]{:S(2)}) copy-start(f32[4,3,512]{2,0,1:T(4,128)} %param.11) | copy-start | bytes 73732

commit v2 on v1

--- a/solution.py
+++ b/solution.py
@@ -166,10 +166,11 @@
     new_pos_ref, new_mom_ref,
     first_pos, first_vel, inv_ref, factor_ref, mass_rows, weight, kick, acc, ghost_acc,
     begin, kicks, zg_out, zg_in, part_line, part_out, part_in, q_own, qg_out, qg_in, piece,
-    free_out, free_in, edge_out, edge_in,
+    free_out, free_in, edge_out, edge_in, side_out, side_in, side_sum, found_near, found_q,
+    inv_row,
     pos_ref, mom_ref, near_ref, ghost_ref, species_ref, scale_ref, mass_ref, w_in_ref, w_out_ref,
     table_ref, load_s, zg_s, zg_r, part_s, part_r, begin_s, begin_r, qg_s, qg_r, kick_s, kick_r,
-    piece_s, piece_r, free_s, free_r, edge_s, edge_r,
+    piece_s, piece_r, free_s, free_r, edge_s, edge_r, side_s, side_r,
 ):
     _, per_device, atoms = pos_ref.shape
     slots = near_ref.shape[0]
@@ -241,6 +242,13 @@
             device_id={"bead": peers[j], "space": (above, below)[side]}, device_id_type=MESH,
         )
 
+    def to_piece_edge(side, j, sender):
+        return pltpu.make_async_remote_copy(
+            src_ref=side_out.at[side], dst_ref=side_in.at[side, sender],
+            send_sem=side_s.at[side, j], recv_sem=side_r.at[side, j],
+            device_id={"bead": peers[j], "space": (above, below)[side]}, device_id_type=MESH,
+        )
+
     sent = []
 
     def start(copies):
@@ -308,6 +316,7 @@
         mass = jnp.where(species == kind, mass_ref[0:1, kind : kind + 1], mass)
     inverse = 1.0 / mass
     factor_ref[...] = charge * inverse
+    inv_row[...] = inverse
 
     if used < TILE:
         first_pos[...] = jnp.zeros(first_pos.shape, jnp.float32)
@@ -358,97 +367,105 @@
             for c in range(3):
                 first_vel[at, lane_of(s, c)] = mom_ref[c, :, chunk] * own
 
-    await_blocks(part_in, part_s, part_r)
-    contracted = part_out[member]
-    for j in order:
-        contracted = contracted + part_in[peers[j]]
-    part_line[0 : contracted.shape[0], 0:LANES] = contracted
-
-    def put_q(value_of):
-        for i in range(3):
-            for m in range(atom_chunks):
-                q_own[i : i + 1, chunk_of(m)] = value_of(i, m)
-
-    put_q(lambda i, m: part_line[i * atom_chunks + m : i * atom_chunks + m + 1, 0:LANES])
-    for side in range(2):
-        low, high = index_of(side)
-        qg_out[side] = pick([q_own[:, chunk_of(m)] for m in range(atom_chunks)], low, high)
-    qcopies = [to_side(qg_out.at[side], qg_in.at[side], qg_s, qg_r, side) for side in range(2)]
-    start(qcopies)
-    for load in loads[7:]:
-        load.wait()
-    for copy in ghost_copies:
-        copy.wait_recv()
-
     def ghost_row(ref, lead, side, c, b):
         at = c // groups_of * TILE + c % groups_of * per_device + b
         return spread_row(ref[(*lead, side, slice(at, at + 1), slice(None))])
 
-    chunks = [ghost_row(zg_in, (0,), 0, 3, 0)]
-    chunks += [spread_row(charge[:, chunk_of(m)]) for m in range(atom_chunks)]
-    chunks += [ghost_row(zg_in, (0,), 1, 3, 0)]
-    for m in range(atom_chunks):
-        itself = ghosts + m * LANES + lax.broadcasted_iota(jnp.int32, (TILE, LANES), 1)
-        for k in range(0, slots, TILE):
-            index = near_ref[k : k + TILE, chunk_of(m)]
-            value = pick(chunks, index & (LANES - 1), index // LANES)
-            weight[k : k + TILE, chunk_of(m)] = jnp.where(index == itself, 0.0, value)
+    def own_row(ref, lead, m, c, b):
+        at = m // strips * per_device + b
+        return spread_row(ref[(*lead, slice(at, at + 1), lane_of(m % strips, c))])
+
+    def near_tiles(lanes):
+        indices = [near_ref[k : k + TILE, lanes] for k in range(0, slots, TILE)]
+        return [index & (LANES - 1) for index in indices], [index // LANES for index in indices]
+
+    def pick_own(sources, low, high):
+        found = lookup(sources[0], low)
+        for m in range(1, atom_chunks):
+            found = jnp.where(high == 1 + m, lookup(sources[m], low), found)
+        return found
+
+    def pick_ghost(sides, found, low, high):
+        found = jnp.where(high == 0, lookup(sides[0], low), found)
+        return jnp.where(high == 1 + atom_chunks, lookup(sides[1], low), found)
+
+    slot_tiles = slots // TILE
+
+    def found_at(m, b, c, t):
+        at = (((m * per_device + b) * 3 + c) * slot_tiles + t) * TILE
+        return slice(at, at + TILE)
+
+    def cheap_own(own_ref, own_lead):
+        for m in range(atom_chunks):
+            lows, highs = near_tiles(chunk_of(m))
+            for t in range(slot_tiles):
+                for b in range(per_device):
+                    for c in range(3):
+                        sources = [own_row(own_ref, own_lead, k, c, b) for k in range(atom_chunks)]
+                        found_near[found_at(m, b, c, t), :] = pick_own(sources, lows[t], highs[t])
 
     def cheap(own_ref, own_lead, ghost_ref_of, ghost_lead, finish):
         for s in range(strips):
             for h in range(halves):
-                lanes = chunk_of(h * strips + s)
+                m = h * strips + s
+                lanes = chunk_of(m)
                 factor = factor_ref[:, lanes]
-                indices = [near_ref[k : k + TILE, lanes] for k in range(0, slots, TILE)]
-                lows = [index & (LANES - 1) for index in indices]
-                highs = [index // LANES for index in indices]
+                lows, highs = near_tiles(lanes)
+                totals = [[None] * 3 for _ in range(per_device)]
+                for t in range(slot_tiles):
+                    pull = weight[t * TILE : (t + 1) * TILE, lanes]
+                    for b in range(per_device):
+                        offsets = []
+                        for c in range(3):
+                            sides = [
+                                ghost_row(ghost_ref_of, ghost_lead, side, c, b) for side in range(2)
+                            ]
+                            found = found_near[found_at(m, b, c, t), :]
+                            offsets.append(
+                                pick_ghost(sides, found, lows[t], highs[t])
+                                - own_row(own_ref, own_lead, m, c, b)
+                            )
+                        squared = sum(offset * offset for offset in offsets)
+                        strength = pull * jnp.exp(-squared / pair_width)
+                        for c in range(3):
+                            term = strength * offsets[c]
+                            totals[b][c] = term if t == 0 else totals[b][c] + term
                 for b in range(per_device):
-                    offsets = []
-                    for c in range(3):
-                        def own_row(m):
-                            at = m // strips * per_device + b
-                            return spread_row(
-                                own_ref[(*own_lead, slice(at, at + 1), lane_of(m % strips, c))]
-                            )
-                        sources = [ghost_row(ghost_ref_of, ghost_lead, 0, c, b)]
-                        sources += [own_row(m) for m in range(atom_chunks)]
-                        sources += [ghost_row(ghost_ref_of, ghost_lead, 1, c, b)]
-                        middle = own_row(h * strips + s)
-                        offsets.append(
-                            [pick(sources, low, high) - middle for low, high in zip(lows, highs)]
-                        )
-                    totals = [None] * 3
-                    for t in range(len(indices)):
-                        squared = sum(offsets[c][t] * offsets[c][t] for c in range(3))
-                        strength = weight[t * TILE : (t + 1) * TILE, lanes] * jnp.exp(
-                            -squared / pair_width
-                        )
-                        for c in range(3):
-                            term = strength * offsets[c][t]
-                            totals[c] = term if totals[c] is None else totals[c] + term
                     at = h * per_device + b
                     for c in range(3):
-                        total = jnp.sum(totals[c], axis=0, keepdims=True)
+                        total = jnp.sum(totals[b][c], axis=0, keepdims=True)
                         kick[at : at + 1, lane_of(s, c)] = pair_strength * factor * total
             finish(s)
 
+    def share_lanes(t):
+        return pl.ds(pl.multiple_of(first + t * LANES, LANES), LANES)
+
+    def q_at(t, c, k):
+        at = ((t * 3 + c) * slot_tiles + k) * TILE
+        return slice(at, at + TILE)
+
+    def learned_own():
+        for t in range(cover // LANES):
+            lows, highs = near_tiles(share_lanes(t))
+            for k in range(slot_tiles):
+                for c in range(3):
+                    sources = [spread_row(q_own[c : c + 1, chunk_of(m)]) for m in range(atom_chunks)]
+                    found_q[q_at(t, c, k), :] = pick_own(sources, lows[k], highs[k])
+
     def learned(low_high, slot):
         rates = radial_rates(w_in_ref.shape[0])
+        forces = []
         for t in range(cover // LANES):
-            lanes = pl.ds(pl.multiple_of(first + t * LANES, LANES), LANES)
-            indices = [near_ref[k : k + TILE, lanes] for k in range(0, slots, TILE)]
-            offsets = []
-            for c in range(3):
-                low, high = low_high(c)
-                own = [spread_row(q_own[c : c + 1, chunk_of(m)]) for m in range(atom_chunks)]
-                chunks = [low] + own + [high]
-                middle = spread_row(q_own[c : c + 1, lanes])
-                offsets.append(
-                    [pick(chunks, index & (LANES - 1), index // LANES) - middle for index in indices]
-                )
+            lanes = share_lanes(t)
+            lows, highs = near_tiles(lanes)
+            offsets = [[None] * slot_tiles for _ in range(3)]
+            for k in range(slot_tiles):
+                for c in range(3):
+                    found = pick_ghost(low_high(c), found_q[q_at(t, c, k), :], lows[k], highs[k])
+                    offsets[c][k] = found - spread_row(q_own[c : c + 1, lanes])
             bases = []
             messages = [None] * len(rates)
-            for k in range(len(indices)):
+            for k in range(slot_tiles):
                 squared = sum(offsets[c][k] * offsets[c][k] for c in range(3))
                 basis = [jnp.exp(-float(rates[r]) * squared) for r in range(2)]
                 for r in range(2, len(rates)):
@@ -469,7 +486,7 @@
             radial = dot(w_out_ref[...], hidden)
             spread_radial = [spread_row(radial[r : r + 1, :]) for r in range(len(rates))]
             totals = [None] * 3
-            for k in range(len(indices)):
+            for k in range(slot_tiles):
                 profile = sum(spread_radial[r] * bases[k][r] for r in range(len(rates)))
                 strength = weight[k * TILE : (k + 1) * TILE, lanes] * profile
                 for c in range(3):
@@ -479,11 +496,24 @@
             for c in range(3):
                 total = spread_row(jnp.sum(totals[c], axis=0, keepdims=True))
                 tile = jnp.where(row_at % 4 == c, total, tile)
+            forces.append(tile)
             tile = jnp.where(row_at // 4 == t % 2, tile, 0.0)
             at = t // 2 * TILE
             if t % 2:
                 tile = tile + piece[slot, me, at : at + TILE, :]
             piece[slot, me, at : at + TILE, :] = tile
+        if slot == 0:
+            begins = lax.rem(me, groups) * share
+            for side in range(2):
+                index = spread_row(ghost_ref[1 - side : 2 - side, :])
+                low, high = index & (LANES - 1), index // LANES
+                value = jnp.zeros((TILE, LANES), jnp.float32)
+                for t in range(cover // LANES):
+                    force = forces[t] * spread_row(inv_row[:, share_lanes(t)])
+                    value = jnp.where(high == first // LANES + t, lookup(force, low), value)
+                value = jnp.where((index >= begins) & (index < begins + share), value, 0.0)
+                side_out[side] = value[0:4]
+            start([to_piece_edge(side, j, me) for j in order + [0] for side in range(2)])
         start([
             to_peer(piece.at[slot, me], piece.at[slot, me], piece_s.at[slot], piece_r.at[slot], j)
             for j in order
@@ -537,29 +567,98 @@
     for step in range(NINNER):
         step_row.append(step_row[-1] + (KINDS - step) * TILE)
 
+    free_kinds = ((0, per_device), (1, per_device), (2, per_device), (4, 1))
+
+    def send_edges(step):
+        if step == 0:
+            kick[...] = kicks[0, me]
+        for side in range(2):
+            tiles = compose(ghost_values(kick, (), side, per_device), per_device)
+            for t, tile in enumerate(tiles):
+                rows = min(TILE, 3 * per_device - t * TILE)
+                edge_out[step, side, t * TILE : t * TILE + rows, :] = tile[0:rows]
+        start([to_edge(step, side, j, me) for j in order + [0] for side in range(2)])
+
+    def await_edges(step):
+        for j in order + [0]:
+            for side in range(2):
+                to_edge(step, side, j, peers[j]).wait_recv()
+        if step == 0:
+            for j in order + [0]:
+                for side in range(2):
+                    to_piece_edge(side, j, peers[j]).wait_recv()
+            for side in range(2):
+                for c in range(CB):
+                    total = side_in[side, c * groups]
+                    for part in range(1, groups):
+                        total = total + side_in[side, c * groups + part]
+                    side_sum[side, c] = total
+        lines = []
+        for side in range(2):
+            for t in range(ghost_tiles):
+                rows = min(TILE, 3 * per_device - t * TILE)
+                tiles = []
+                for device in range(devices):
+                    tile = edge_in[step, side, device, t * TILE : t * TILE + rows, :]
+                    if rows < TILE:
+                        tile = jnp.concatenate(
+                            (tile, jnp.zeros((TILE - rows, LANES), jnp.float32)), axis=0
+                        )
+                    tiles.append(tile)
+                if step == 0:
+                    for top in range(0, extra, TILE):
+                        tile = jnp.zeros((TILE, LANES), jnp.float32)
+                        for row in range(top, min(extra, top + TILE)):
+                            i, c = t * groups_of + row // CB, row % CB
+                            if i < 3:
+                                value = spread_row(side_sum[side, c, i : i + 1, :])
+                                tile = jnp.where(row_at == row - top, value, tile)
+                        tiles.append(tile)
+                lines.append(jnp.concatenate(tiles, axis=0))
+        return jnp.concatenate(lines, axis=1)
+
+    for load in loads[7:]:
+        load.wait()
+    cheap_own(first_pos, ())
+    await_blocks(part_in, part_s, part_r)
+    contracted = part_out[member]
+    for j in order:
+        contracted = contracted + part_in[peers[j]]
+    part_line[0 : contracted.shape[0], 0:LANES] = contracted
+
+    def put_q(value_of):
+        for i in range(3):
+            for m in range(atom_chunks):
+                q_own[i : i + 1, chunk_of(m)] = value_of(i, m)
+
+    put_q(lambda i, m: part_line[i * atom_chunks + m : i * atom_chunks + m + 1, 0:LANES])
+    for side in range(2):
+        low, high = index_of(side)
+        qg_out[side] = pick([q_own[:, chunk_of(m)] for m in range(atom_chunks)], low, high)
+    qcopies = [to_side(qg_out.at[side], qg_in.at[side], qg_s, qg_r, side) for side in range(2)]
+    start(qcopies)
+    learned_own()
+    for copy in ghost_copies:
+        copy.wait_recv()
+
+    chunks = [ghost_row(zg_in, (0,), 0, 3, 0)]
+    chunks += [spread_row(charge[:, chunk_of(m)]) for m in range(atom_chunks)]
+    chunks += [ghost_row(zg_in, (0,), 1, 3, 0)]
+    for m in range(atom_chunks):
+        itself = ghosts + m * LANES + lax.broadcasted_iota(jnp.int32, (TILE, LANES), 1)
+        for k in range(0, slots, TILE):
+            index = near_ref[k : k + TILE, chunk_of(m)]
+            value = pick(chunks, index & (LANES - 1), index // LANES)
+            weight[k : k + TILE, chunk_of(m)] = jnp.where(index == itself, 0.0, value)
+
     cheap(first_pos, (), zg_in, (0,), send_kick(0))
+    send_edges(0)
     await_blocks(begin, begin_s, begin_r)
     based = dot(table_ref[base_row : base_row + KINDS * TILE, 0:width], begin[...].reshape(width, -1))
-    for copy in qcopies:
-        copy.wait_recv()
-    learned(lambda c: [spread_row(qg_in[side, c : c + 1, :]) for side in range(2)], 0)
-    await_kick(0)
-    await_blocks(piece.at[0], piece_s.at[0], piece_r.at[0])
-    every = jnp.concatenate((kicks[0].reshape(width, -1), all_pieces(0, inverse)), axis=0)
-    based = based + dot(table_ref[step_row[0] : step_row[1], 0 : width + extra], every)
     for kind in range(KINDS):
         acc[kind] = based[kind * TILE : (kind + 1) * TILE, :]
-
     for side in range(2):
-        for t, tile in enumerate(compose(ghost_values(acc, (0,), side, per_device), per_device)):
-            zg_out[1, side, t * TILE : (t + 1) * TILE, :] = tile
-    ghost_copies = [
-        to_side(zg_out.at[1, side], zg_in.at[1, side], zg_s.at[1], zg_r.at[1], side)
-        for side in range(2)
-    ]
-    start(ghost_copies)
-    for side in range(2):
-        for number, (kind, unit) in enumerate(((1, per_device), (2, per_device), (4, 1))):
+        for number, (kind, unit) in enumerate(free_kinds):
             for t, tile in enumerate(compose(ghost_values(acc, (kind,), side, unit), unit)):
                 at = (number * ghost_tiles + t) * TILE
                 free_out[side, at : at + TILE, :] = tile
@@ -567,74 +666,55 @@
         to_side(free_out.at[side], free_in.at[side], free_s, free_r, side) for side in range(2)
     ]
     start(free_copies)
-    for copy in ghost_copies:
+    for copy in qcopies:
         copy.wait_recv()
-
-    def send_edges(step):
-        for side in range(2):
-            tiles = compose(ghost_values(kick, (), side, per_device), per_device)
-            for t, tile in enumerate(tiles):
-                rows = min(TILE, 3 * per_device - t * TILE)
-                edge_out[step - 1, side, t * TILE : t * TILE + rows, :] = tile[0:rows]
-        start([to_edge(step - 1, side, j, me) for j in order + [0] for side in range(2)])
-
-    def await_edges(step):
-        for j in order + [0]:
-            for side in range(2):
-                to_edge(step - 1, side, j, peers[j]).wait_recv()
-        lines = []
-        for side in range(2):
-            for t in range(ghost_tiles):
-                rows = min(TILE, 3 * per_device - t * TILE)
-                tiles = []
-                for device in range(devices):
-                    tile = edge_in[step - 1, side, device, t * TILE : t * TILE + rows, :]
-                    if rows < TILE:
-                        tile = jnp.concatenate(
-                            (tile, jnp.zeros((TILE - rows, LANES), jnp.float32)), axis=0
-                        )
-                    tiles.append(tile)
-                lines.append(jnp.concatenate(tiles, axis=0))
-        return jnp.concatenate(lines, axis=1)
-
-    cheap(acc, (0,), zg_in, (1,), send_kick(1))
-    send_edges(1)
+    learned(lambda c: [spread_row(qg_in[side, c : c + 1, :]) for side in range(2)], 0)
     for copy in free_copies:
         copy.wait_recv()
-    for step in range(1, NINNER):
+
+    for step in range(NINNER):
+        last = step + 1 == NINNER
         await_kick(step)
-        table = table_ref[step_row[step] : step_row[step + 1], 0:width]
-        moved = dot(table, kicks[step].reshape(width, -1))
+        every = kicks[step].reshape(width, -1)
+        depth = width
+        if step == 0:
+            await_blocks(piece.at[0], piece_s.at[0], piece_r.at[0])
+            every = jnp.concatenate((every, all_pieces(0, inverse)), axis=0)
+            depth = width + extra
+        table = table_ref[step_row[step] : step_row[step + 1], 0:depth]
+        moved = dot(table, every)
         for kind in range(step, KINDS):
             at = (kind - step) * TILE
             acc[kind] = acc[kind] + moved[at : at + TILE, :]
+        if last:
+            put_q(lambda i, m: acc[4, m // strips : m // strips + 1, lane_of(m % strips, i)])
+            learned_own()
+        cheap_own(acc, (step,))
         moved = dot(table, await_edges(step))
         for side in range(2):
-            for number, kind in enumerate((1, 2, 4)):
+            for number, (kind, _) in enumerate(free_kinds):
                 if kind < step:
                     continue
                 at = (kind - step) * TILE
                 for t in range(ghost_tiles):
                     line = (side * ghost_tiles + t) * LANES
-                    held = (number * ghost_tiles + t) * TILE
-                    old = free_in if step == 1 else ghost_acc
-                    ghost_acc[side, held : held + TILE, :] = (
-                        old[side, held : held + TILE, :] + moved[at : at + TILE, line : line + LANES]
+                    held = slice((number * ghost_tiles + t) * TILE, (number * ghost_tiles + t + 1) * TILE)
+                    old = free_in if step == 0 else ghost_acc
+                    ghost_acc[side, held, :] = (
+                        old[side, held, :] + moved[at : at + TILE, line : line + LANES]
                     )
-        if step + 1 == NINNER:
-            put_q(lambda i, m: acc[4, m // strips : m // strips + 1, lane_of(m % strips, i)])
-
+        if last:
             def low_high(c):
-                at = (2 * ghost_tiles + c // groups_of) * TILE + c % groups_of
+                at = (3 * ghost_tiles + c // groups_of) * TILE + c % groups_of
                 return [spread_row(ghost_acc[side, at : at + 1, :]) for side in range(2)]
 
             learned(low_high, 1)
-        shifted = ghost_acc.at[:, step_tile(step, ghost_tiles), :]
-        if step + 1 < NINNER:
+        shifted = ghost_acc.at[:, step * ghost_tiles * TILE : (step + 1) * ghost_tiles * TILE, :]
+        if last:
+            cheap(acc, (step,), shifted, (), lambda s: None)
+        else:
             cheap(acc, (step,), shifted, (), send_kick(step + 1))
             send_edges(step + 1)
-        else:
-            cheap(acc, (step,), shifted, (), lambda s: None)
 
     for h in range(halves):
         at = slice(h * per_device, (h + 1) * per_device)
@@ -657,10 +737,6 @@
                 new_mom_ref[c, :, chunk_of(h * strips + s)] = kick[at, lane_of(s, c)]
     for copy in sent:
         copy.wait_send()
-
-
-def step_tile(step, ghost_tiles):
-    return slice((step - 1) * ghost_tiles * TILE, step * ghost_tiles * TILE)
 
 
 def body(
@@ -703,11 +779,11 @@
             pltpu.VMEM((slots, atoms), f32),
             pltpu.VMEM((TILE, lanes), f32),
             pltpu.VMEM((KINDS, TILE, lanes), f32),
-            pltpu.VMEM((2, 3 * ghost_tiles * TILE, ghosts), f32),
+            pltpu.VMEM((2, 4 * ghost_tiles * TILE, ghosts), f32),
             pltpu.VMEM((devices, TILE, lanes), f32),
             pltpu.VMEM((NINNER, devices, TILE, lanes), f32),
-            pltpu.VMEM((2, 2, ghost_tiles * TILE, ghosts), f32),
-            pltpu.VMEM((2, 2, ghost_tiles * TILE, ghosts), f32),
+            pltpu.VMEM((1, 2, ghost_tiles * TILE, ghosts), f32),
+            pltpu.VMEM((1, 2, ghost_tiles * TILE, ghosts), f32),
             pltpu.VMEM((max(extra, lines), lanes), f32),
             pltpu.VMEM((CB, lines, LANES), f32),
             pltpu.VMEM((devices, lines, LANES), f32),
@@ -715,26 +791,33 @@
             pltpu.VMEM((2, TILE, ghosts), f32),
             pltpu.VMEM((2, TILE, ghosts), f32),
             pltpu.VMEM((2, devices, piece_rows, LANES), f32),
-            pltpu.VMEM((2, 3 * ghost_tiles * TILE, ghosts), f32),
-            pltpu.VMEM((2, 3 * ghost_tiles * TILE, ghosts), f32),
-            pltpu.VMEM((NINNER - 1, 2, 3 * per_device, ghosts), f32),
-            pltpu.VMEM((NINNER - 1, 2, devices, 3 * per_device, ghosts), f32),
+            pltpu.VMEM((2, 4 * ghost_tiles * TILE, ghosts), f32),
+            pltpu.VMEM((2, 4 * ghost_tiles * TILE, ghosts), f32),
+            pltpu.VMEM((NINNER, 2, 3 * per_device, ghosts), f32),
+            pltpu.VMEM((NINNER, 2, devices, 3 * per_device, ghosts), f32),
+            pltpu.VMEM((2, 4, ghosts), f32),
+            pltpu.VMEM((2, devices, 4, ghosts), f32),
+            pltpu.VMEM((2, CB, 4, ghosts), f32),
+            pltpu.VMEM((atoms // LANES * per_device * 3 * slots, LANES), f32),
+            pltpu.VMEM((cover // LANES * 3 * slots, LANES), f32),
+            pltpu.VMEM((1, atoms), f32),
             *[pltpu.VMEM(operand.shape, operand.dtype) for operand in operands[:-1]],
             pltpu.VMEM(table.shape[1:], f32),
             dma((len(operands),)),
-            dma((2, 2)), dma((2, 2)),
+            dma((1, 2)), dma((1, 2)),
             dma((devices,)), dma((devices,)),
             dma((devices,)), dma((devices,)),
             dma((2,)), dma((2,)),
             dma((NINNER, strips, devices)), dma((NINNER, strips, devices)),
             dma((2, devices)), dma((2, devices)),
             dma((2,)), dma((2,)),
-            dma((NINNER - 1, 2, devices)), dma((NINNER - 1, 2, devices)),
+            dma((NINNER, 2, devices)), dma((NINNER, 2, devices)),
+            dma((2, devices)), dma((2, devices)),
         ],
         compiler_params=pltpu.CompilerParams(
             collective_id=0, has_side_effects=True, vmem_limit_bytes=16777216
         ),
-    )(*operands)
+    )(*[pltpu.with_memory_space_constraint(x, pltpu.HBM) for x in operands])
     return (new_positions.transpose(1, 0, 2), new_momenta.transpose(1, 0, 2))
 
 

time: 48.7 us -> 41 us (0.84)
  local copies, waits for them, and re-layouts: 5.31 us -> 1.22 us
  Pallas kernels: 42.3 us -> 38.9 us
    unnamed x22 -> x2, local copies, waits for them, and re-layouts: 5.31 us -> 1.22 us
    pallas_call x1, Pallas kernels: 42.3 us -> 38.9 us  [body(): pl.pallas_call(cycle_kernel, name='cycle', out_shape=(shape, shape), in_s...]
where the time goes in v2:
time: 41 us; the launch traced here: 40.8 us
  Pallas kernels  38.9 us (95%)
  local copies, waits for them, and re-layouts  1.22 us (3%)
  between operations  0.64 us (2%)
    pallas_call x1, Pallas kernels, body(): pl.pallas_call(cycle_kernel, name='cycle', out_shape=(shape, shape), in_s...  38.9 us
    unnamed x2, local copies, waits for them, and re-layouts  1.22 us

profile of v2, /device:TPU:0, one launch (start us, length us, event | category | flops | bytes accessed | tf_op | source)
XLA Modules:
  0.0 40.8 jit_solution(13292394407038137198)
XLA Ops:
  0.6 38.9 %cycle.1 = (f32[3,4,512]{2,1,0:T(4,128)S(1)}, f32[3,4,512]{2,1,0:T(4,128)S(1)}) custom-call(f32[3,4,512]{2,1,0:T(4,128)} %bitcast.11, f32[3,4,512]{2,1,0:T(4,128)} %bitcast.12, s32[32,512]{1,0:T(8,128)} %near_in.1, s32[2,128]{1,0:T(2,128)} %bitcast.15, s32[1,512]{1,0:T(1,128)} %bitcast.14, f32[1,2]{1,0:T(1,128)} %bitcast.16, f32[1,2]{1,0:T(1,128)} %bitcast.17, ...), custom_call_target="tpu_custom_call" | custom-call | tf_op jit(solution)/shard_map/cycle/pallas_call | solution.py:767
  39.6 0.6 %copy.14 = f32[4,3,512]{2,0,1:T(4,128)} copy(f32[4,3,512]{2,0,1:T(4,128)S(1)} %bitcast.10) | data formatting | bytes 49152
  40.2 0.6 %copy.15 = f32[4,3,512]{2,0,1:T(4,128)} copy(f32[4,3,512]{2,0,1:T(4,128)S(1)} %bitcast.9) | data formatting | bytes 49152

commit v3 on v2

--- a/solution.py
+++ b/solution.py
@@ -163,14 +163,13 @@
 
 def cycle_kernel(
     pos_in, mom_in, near_in, ghost_from, species_in, scale_in, mass_in, w_in_in, w_out_in, table_in,
-    new_pos_ref, new_mom_ref,
+    new_ref,
     first_pos, first_vel, inv_ref, factor_ref, mass_rows, weight, kick, acc, ghost_acc,
     begin, kicks, zg_out, zg_in, part_line, part_out, part_in, q_own, qg_out, qg_in, piece,
     free_out, free_in, edge_out, edge_in, side_out, side_in, side_sum, found_near, found_q,
     inv_row,
     pos_ref, mom_ref, near_ref, ghost_ref, species_ref, scale_ref, mass_ref, w_in_ref, w_out_ref,
-    table_ref, load_s, zg_s, zg_r, part_s, part_r, begin_s, begin_r, qg_s, qg_r, kick_s, kick_r,
-    piece_s, piece_r, free_s, free_r, edge_s, edge_r, side_s, side_r,
+    table_ref, load_s, send_s, recv_s,
 ):
     _, per_device, atoms = pos_ref.shape
     slots = near_ref.shape[0]
@@ -223,42 +222,37 @@
     for target in (above, below):
         pl.semaphore_signal(barrier, inc=1, device_id={"space": target}, device_id_type=MESH)
 
-    def to_peer(src, dst, send, recv, j):
+    ghost_at, part_at, begin_at, qghost_at, free_at, side_at = range(6)
+    piece_at, kick_at, edge_at = 6, 8, 8 + NINNER
+    sent = []
+
+    def remote(src, dst, phase, where):
         return pltpu.make_async_remote_copy(
-            src_ref=src, dst_ref=dst, send_sem=send.at[j], recv_sem=recv.at[j],
-            device_id={"bead": peers[j]}, device_id_type=MESH,
+            src_ref=src, dst_ref=dst, send_sem=send_s.at[phase], recv_sem=recv_s.at[phase],
+            device_id=where, device_id_type=MESH,
         )
 
-    def to_side(src, dst, send, recv, side):
-        return pltpu.make_async_remote_copy(
-            src_ref=src, dst_ref=dst, send_sem=send.at[side], recv_sem=recv.at[side],
-            device_id={"space": (above, below)[side]}, device_id_type=MESH,
-        )
-
-    def to_edge(step, side, j, sender):
-        return pltpu.make_async_remote_copy(
-            src_ref=edge_out.at[step, side], dst_ref=edge_in.at[step, side, sender],
-            send_sem=edge_s.at[step, side, j], recv_sem=edge_r.at[step, side, j],
-            device_id={"bead": peers[j], "space": (above, below)[side]}, device_id_type=MESH,
-        )
-
-    def to_piece_edge(side, j, sender):
-        return pltpu.make_async_remote_copy(
-            src_ref=side_out.at[side], dst_ref=side_in.at[side, sender],
-            send_sem=side_s.at[side, j], recv_sem=side_r.at[side, j],
-            device_id={"bead": peers[j], "space": (above, below)[side]}, device_id_type=MESH,
-        )
-
-    sent = []
-
-    def start(copies):
-        for copy in copies:
-            copy.start()
-            sent.append(copy)
-
-    def await_blocks(buffer, send, recv):
+    def send_peers(src_of, dst, phase):
         for j in order:
-            to_peer(buffer.at[peers[j]], buffer.at[peers[j]], send, recv, j).wait_recv()
+            remote(src_of(j), dst, phase, {"bead": peers[j]}).start()
+
+    def send_sides(src, dst, phase):
+        for side in range(2):
+            remote(src.at[side], dst.at[side], phase, {"space": (above, below)[side]}).start()
+
+    def send_around(src, dst, phase):
+        for j in order + [0]:
+            for side in range(2):
+                where = {"bead": peers[j], "space": (above, below)[side]}
+                remote(src.at[side], dst.at[side, me], phase, where).start()
+
+    def arrived(block, phase):
+        whole = remote(block, block, phase, {"space": above})
+        whole.wait_recv()
+        sent.append(whole)
+
+    def others(buffer):
+        return buffer.at[0 : devices - 1]
 
     row_at = lax.broadcasted_iota(jnp.int32, (TILE, LANES), 0)
 
@@ -337,7 +331,7 @@
         parts = [spread_row(charge[:, chunk_of(m)]) for m in range(atom_chunks)]
         values = ghost_values(first_pos, (), side, per_device) + [pick(parts, low, high)]
         for t, tile in enumerate(compose(values, per_device)):
-            zg_out[0, side, t * TILE : (t + 1) * TILE, :] = tile
+            zg_out[side, t * TILE : (t + 1) * TILE, :] = tile
 
     part_line[0:extra, :] = dot(table_ref[0:extra, 0:TILE], first_pos[...])
     for c in range(CB):
@@ -349,13 +343,9 @@
                 part_out[c, at : at + 1, :] = part_line[row : row + 1, lane_of(s, i)]
 
     pl.semaphore_wait(barrier, devices + 1)
-    ghost_copies = [
-        to_side(zg_out.at[0, side], zg_in.at[0, side], zg_s.at[0], zg_r.at[0], side)
-        for side in range(2)
-    ]
-    start(ghost_copies)
-    start([to_peer(part_out.at[peers[j] // groups], part_in.at[me], part_s, part_r, j) for j in order])
-    start([to_peer(begin.at[me], begin.at[me], begin_s, begin_r, j) for j in order])
+    send_sides(zg_out, zg_in, ghost_at)
+    send_peers(lambda j: part_out.at[peers[j] // groups], part_in.at[me], part_at)
+    send_peers(lambda j: begin.at[me], begin.at[me], begin_at)
 
     for h in range(halves):
         at = slice(h * per_device, (h + 1) * per_device)
@@ -454,7 +444,7 @@
 
     def learned(low_high, slot):
         rates = radial_rates(w_in_ref.shape[0])
-        forces = []
+        forces, lines, held = [], [], []
         for t in range(cover // LANES):
             lanes = share_lanes(t)
             lows, highs = near_tiles(lanes)
@@ -475,15 +465,20 @@
                 for r in range(len(rates)):
                     term = strength * basis[r]
                     messages[r] = term if messages[r] is None else messages[r] + term
-            message = jnp.concatenate(
+            lines.append(jnp.concatenate(
                 [jnp.sum(m, axis=0, keepdims=True) for m in messages], axis=0
-            ) / slots
-            hidden = lax.dot_general(
-                w_in_ref[...], message, (((0,), (0,)), ((), ())),
-                precision=highest, preferred_element_type=jnp.float32,
-            )
-            hidden = hidden * jax.nn.sigmoid(hidden)
-            radial = dot(w_out_ref[...], hidden)
+            ) / slots)
+            held.append((offsets, bases))
+        hidden = lax.dot_general(
+            w_in_ref[...], jnp.concatenate(lines, axis=1), (((0,), (0,)), ((), ())),
+            precision=highest, preferred_element_type=jnp.float32,
+        )
+        hidden = hidden * jax.nn.sigmoid(hidden)
+        radials = dot(w_out_ref[...], hidden)
+        for t in range(cover // LANES):
+            lanes = share_lanes(t)
+            offsets, bases = held[t]
+            radial = radials[:, t * LANES : (t + 1) * LANES]
             spread_radial = [spread_row(radial[r : r + 1, :]) for r in range(len(rates))]
             totals = [None] * 3
             for k in range(slot_tiles):
@@ -513,11 +508,8 @@
                     value = jnp.where(high == first // LANES + t, lookup(force, low), value)
                 value = jnp.where((index >= begins) & (index < begins + share), value, 0.0)
                 side_out[side] = value[0:4]
-            start([to_piece_edge(side, j, me) for j in order + [0] for side in range(2)])
-        start([
-            to_peer(piece.at[slot, me], piece.at[slot, me], piece_s.at[slot], piece_r.at[slot], j)
-            for j in order
-        ])
+            send_around(side_out, side_in, side_at)
+        send_peers(lambda j: piece.at[slot, me], piece.at[slot, me], piece_at + slot)
 
     def all_pieces(slot, scale):
         line = []
@@ -548,19 +540,9 @@
             else:
                 kick[:, lanes] = inner_step * kick[:, lanes]
                 kicks[step, me, :, lanes] = kick[:, lanes]
-            start([
-                to_peer(kicks.at[step, me, :, lanes], kicks.at[step, me, :, lanes],
-                        kick_s.at[step, s], kick_r.at[step, s], j)
-                for j in order
-            ])
+            strip = kicks.at[step, me, :, lanes]
+            send_peers(lambda j: strip, strip, kick_at + step)
         return finish
-
-    def await_kick(step):
-        for s in range(strips):
-            lanes = slice(s * wide, (s + 1) * wide)
-            for j in order:
-                block = kicks.at[step, peers[j], :, lanes]
-                to_peer(block, block, kick_s.at[step, s], kick_r.at[step, s], j).wait_recv()
 
     base_row = extra + TILE
     step_row = [base_row + KINDS * TILE]
@@ -577,16 +559,13 @@
             for t, tile in enumerate(tiles):
                 rows = min(TILE, 3 * per_device - t * TILE)
                 edge_out[step, side, t * TILE : t * TILE + rows, :] = tile[0:rows]
-        start([to_edge(step, side, j, me) for j in order + [0] for side in range(2)])
+        send_around(edge_out.at[step], edge_in.at[step], edge_at + step)
 
     def await_edges(step):
-        for j in order + [0]:
-            for side in range(2):
-                to_edge(step, side, j, peers[j]).wait_recv()
+        arrived(edge_in.at[step], edge_at + step)
         if step == 0:
-            for j in order + [0]:
-                for side in range(2):
-                    to_piece_edge(side, j, peers[j]).wait_recv()
+            arrived(side_in, side_at)
+            arrived(free_in, free_at)
             for side in range(2):
                 for c in range(CB):
                     total = side_in[side, c * groups]
@@ -620,7 +599,7 @@
     for load in loads[7:]:
         load.wait()
     cheap_own(first_pos, ())
-    await_blocks(part_in, part_s, part_r)
+    arrived(others(part_in), part_at)
     contracted = part_out[member]
     for j in order:
         contracted = contracted + part_in[peers[j]]
@@ -635,15 +614,13 @@
     for side in range(2):
         low, high = index_of(side)
         qg_out[side] = pick([q_own[:, chunk_of(m)] for m in range(atom_chunks)], low, high)
-    qcopies = [to_side(qg_out.at[side], qg_in.at[side], qg_s, qg_r, side) for side in range(2)]
-    start(qcopies)
+    send_sides(qg_out, qg_in, qghost_at)
     learned_own()
-    for copy in ghost_copies:
-        copy.wait_recv()
-
-    chunks = [ghost_row(zg_in, (0,), 0, 3, 0)]
+    arrived(zg_in, ghost_at)
+
+    chunks = [ghost_row(zg_in, (), 0, 3, 0)]
     chunks += [spread_row(charge[:, chunk_of(m)]) for m in range(atom_chunks)]
-    chunks += [ghost_row(zg_in, (0,), 1, 3, 0)]
+    chunks += [ghost_row(zg_in, (), 1, 3, 0)]
     for m in range(atom_chunks):
         itself = ghosts + m * LANES + lax.broadcasted_iota(jnp.int32, (TILE, LANES), 1)
         for k in range(0, slots, TILE):
@@ -651,9 +628,9 @@
             value = pick(chunks, index & (LANES - 1), index // LANES)
             weight[k : k + TILE, chunk_of(m)] = jnp.where(index == itself, 0.0, value)
 
-    cheap(first_pos, (), zg_in, (0,), send_kick(0))
+    cheap(first_pos, (), zg_in, (), send_kick(0))
     send_edges(0)
-    await_blocks(begin, begin_s, begin_r)
+    arrived(others(begin), begin_at)
     based = dot(table_ref[base_row : base_row + KINDS * TILE, 0:width], begin[...].reshape(width, -1))
     for kind in range(KINDS):
         acc[kind] = based[kind * TILE : (kind + 1) * TILE, :]
@@ -662,23 +639,17 @@
             for t, tile in enumerate(compose(ghost_values(acc, (kind,), side, unit), unit)):
                 at = (number * ghost_tiles + t) * TILE
                 free_out[side, at : at + TILE, :] = tile
-    free_copies = [
-        to_side(free_out.at[side], free_in.at[side], free_s, free_r, side) for side in range(2)
-    ]
-    start(free_copies)
-    for copy in qcopies:
-        copy.wait_recv()
+    send_sides(free_out, free_in, free_at)
+    arrived(qg_in, qghost_at)
     learned(lambda c: [spread_row(qg_in[side, c : c + 1, :]) for side in range(2)], 0)
-    for copy in free_copies:
-        copy.wait_recv()
 
     for step in range(NINNER):
         last = step + 1 == NINNER
-        await_kick(step)
+        arrived(others(kicks.at[step]), kick_at + step)
         every = kicks[step].reshape(width, -1)
         depth = width
         if step == 0:
-            await_blocks(piece.at[0], piece_s.at[0], piece_r.at[0])
+            arrived(others(piece.at[0]), piece_at)
             every = jnp.concatenate((every, all_pieces(0, inverse)), axis=0)
             depth = width + extra
         table = table_ref[step_row[step] : step_row[step + 1], 0:depth]
@@ -720,8 +691,10 @@
         at = slice(h * per_device, (h + 1) * per_device)
         for s in range(strips):
             for c in range(3):
-                new_pos_ref[c, :, chunk_of(h * strips + s)] = acc[2, at, lane_of(s, c)]
-    await_blocks(piece.at[1], piece_s.at[1], piece_r.at[1])
+                new_ref[0, c, :, chunk_of(h * strips + s)] = acc[2, at, lane_of(s, c)]
+    for copy in sent:
+        copy.wait_send()
+    arrived(others(piece.at[1]), piece_at + 1)
     slow = dot(table_ref[extra : extra + TILE, 0:extra], all_pieces(1, None))
     for s in range(strips):
         heavy = mass_rows[:, chunk_of(s)]
@@ -734,9 +707,8 @@
         at = slice(h * per_device, (h + 1) * per_device)
         for s in range(strips):
             for c in range(3):
-                new_mom_ref[c, :, chunk_of(h * strips + s)] = kick[at, lane_of(s, c)]
-    for copy in sent:
-        copy.wait_send()
+                new_ref[1, c, :, chunk_of(h * strips + s)] = kick[at, lane_of(s, c)]
+    sent[-1].wait_send()
 
 
 def body(
@@ -763,13 +735,13 @@
         ghost_rows.reshape(2, ghosts), species.reshape(1, atoms), species_scale.reshape(1, -1),
         mass_table.reshape(1, -1), w_in.T, w_out, table,
     )
-    shape = jax.ShapeDtypeStruct(operands[0].shape, f32)
-    new_positions, new_momenta = pl.pallas_call(
+    shape = jax.ShapeDtypeStruct((2, *operands[0].shape), f32)
+    new = pl.pallas_call(
         cycle_kernel,
         name="cycle",
-        out_shape=(shape, shape),
+        out_shape=shape,
         in_specs=[hbm] * 10,
-        out_specs=(vmem, vmem),
+        out_specs=vmem,
         scratch_shapes=[
             pltpu.VMEM((TILE, lanes), f32),
             pltpu.VMEM((TILE, lanes), f32),
@@ -782,8 +754,8 @@
             pltpu.VMEM((2, 4 * ghost_tiles * TILE, ghosts), f32),
             pltpu.VMEM((devices, TILE, lanes), f32),
             pltpu.VMEM((NINNER, devices, TILE, lanes), f32),
-            pltpu.VMEM((1, 2, ghost_tiles * TILE, ghosts), f32),
-            pltpu.VMEM((1, 2, ghost_tiles * TILE, ghosts), f32),
+            pltpu.VMEM((2, ghost_tiles * TILE, ghosts), f32),
+            pltpu.VMEM((2, ghost_tiles * TILE, ghosts), f32),
             pltpu.VMEM((max(extra, lines), lanes), f32),
             pltpu.VMEM((CB, lines, LANES), f32),
             pltpu.VMEM((devices, lines, LANES), f32),
@@ -804,21 +776,13 @@
             *[pltpu.VMEM(operand.shape, operand.dtype) for operand in operands[:-1]],
             pltpu.VMEM(table.shape[1:], f32),
             dma((len(operands),)),
-            dma((1, 2)), dma((1, 2)),
-            dma((devices,)), dma((devices,)),
-            dma((devices,)), dma((devices,)),
-            dma((2,)), dma((2,)),
-            dma((NINNER, strips, devices)), dma((NINNER, strips, devices)),
-            dma((2, devices)), dma((2, devices)),
-            dma((2,)), dma((2,)),
-            dma((NINNER, 2, devices)), dma((NINNER, 2, devices)),
-            dma((2, devices)), dma((2, devices)),
+            dma((8 + 2 * NINNER,)), dma((8 + 2 * NINNER,)),
         ],
         compiler_params=pltpu.CompilerParams(
             collective_id=0, has_side_effects=True, vmem_limit_bytes=16777216
         ),
     )(*[pltpu.with_memory_space_constraint(x, pltpu.HBM) for x in operands])
-    return (new_positions.transpose(1, 0, 2), new_momenta.transpose(1, 0, 2))
+    return (new[0].transpose(1, 0, 2), new[1].transpose(1, 0, 2))
 
 
 def solution(mesh):

time: 41 us -> 37.5 us (0.915)
  Pallas kernels: 38.9 us -> 36.1 us
  local copies, waits for them, and re-layouts: 1.22 us -> 0.62 us
    pallas_call x1, Pallas kernels: 38.9 us -> 36.1 us  [body(): pl.pallas_call(cycle_kernel, name='cycle', out_shape=shape, in_specs=[hbm...]
    unnamed x2 -> x0, local copies, waits for them, and re-layouts: 1.22 us -> none
    transpose x0 -> x1, local copies, waits for them, and re-layouts: none -> 0.62 us  [body(): return (new[0].transpose(1, 0, 2), new[1].transpose(1, 0, 2))]
where the time goes in v3:
time: 37.5 us; the launch traced here: 37.3 us
  Pallas kernels  36.1 us (96%)
  between operations  0.64 us (2%)
  local copies, waits for them, and re-layouts  0.62 us (2%)
    pallas_call x1, Pallas kernels, body(): pl.pallas_call(cycle_kernel, name='cycle', out_shape=shape, in_specs=[hbm...  36.1 us

profile of v3, /device:TPU:0, one launch (start us, length us, event | category | flops | bytes accessed | tf_op | source)
XLA Modules:
  0.0 37.3 jit_solution(2117714338331196200)
XLA Ops:
  0.6 36.1 %cycle.1 = f32[2,3,4,512]{3,2,1,0:T(4,128)S(1)} custom-call(f32[3,4,512]{2,1,0:T(4,128)} %bitcast.15, f32[3,4,512]{2,1,0:T(4,128)} %bitcast.16, s32[32,512]{1,0:T(8,128)} %near_in.1, s32[2,128]{1,0:T(2,128)} %bitcast.19, s32[1,512]{1,0:T(1,128)} %bitcast.18, f32[1,2]{1,0:T(1,128)} %bitcast.20, f32[1,2]{1,0:T(1,128)} %bitcast.21, f32[8,128]{1,0:T(8,128)} %bitcast.17, ...), custom_call_target="tpu_custom_call" | custom-call | tf_op jit(solution)/shard_map/cycle/pallas_call | solution.py:739
  36.7 0.6 %slice_bitcast_fusion = (f32[4,3,512]{2,0,1:T(4,128)}, f32[4,3,512]{2,0,1:T(4,128)}) fusion(f32[2,3,4,512]{3,2,1,0:T(4,128)S(1)} %cycle.1), kind=kLoop, calls=%fused_computation | loop fusion | bytes 98304 | tf_op jit(solution)/shard_map/transpose | solution.py:785

commit v4 on v3

--- a/solution.py
+++ b/solution.py
@@ -613,7 +613,7 @@
     put_q(lambda i, m: part_line[i * atom_chunks + m : i * atom_chunks + m + 1, 0:LANES])
     for side in range(2):
         low, high = index_of(side)
-        qg_out[side] = pick([q_own[:, chunk_of(m)] for m in range(atom_chunks)], low, high)
+        qg_out[side] = pick([q_own[:, chunk_of(m)] for m in range(atom_chunks)], low, high)[0:4]
     send_sides(qg_out, qg_in, qghost_at)
     learned_own()
     arrived(zg_in, ghost_at)
@@ -660,7 +660,8 @@
         if last:
             put_q(lambda i, m: acc[4, m // strips : m // strips + 1, lane_of(m % strips, i)])
             learned_own()
-        cheap_own(acc, (step,))
+        else:
+            cheap_own(acc, (step,))
         moved = dot(table, await_edges(step))
         for side in range(2):
             for number, (kind, _) in enumerate(free_kinds):
@@ -682,6 +683,7 @@
             learned(low_high, 1)
         shifted = ghost_acc.at[:, step * ghost_tiles * TILE : (step + 1) * ghost_tiles * TILE, :]
         if last:
+            cheap_own(acc, (step,))
             cheap(acc, (step,), shifted, (), lambda s: None)
         else:
             cheap(acc, (step,), shifted, (), send_kick(step + 1))
@@ -724,7 +726,7 @@
     extra = halves * CB
     lanes = 3 * LANES * strips
     cover = max(atoms // (devices // CB), LANES)
-    lines = -(-3 * (atoms // LANES) // TILE) * TILE
+    lines = 3 * (atoms // LANES)
     piece_rows = -(-(cover // LANES) // 2) * TILE
     vmem = pl.BlockSpec(memory_space=pltpu.VMEM)
     hbm = pl.BlockSpec(memory_space=pltpu.HBM)
@@ -756,12 +758,12 @@
             pltpu.VMEM((NINNER, devices, TILE, lanes), f32),
             pltpu.VMEM((2, ghost_tiles * TILE, ghosts), f32),
             pltpu.VMEM((2, ghost_tiles * TILE, ghosts), f32),
-            pltpu.VMEM((max(extra, lines), lanes), f32),
+            pltpu.VMEM((max(extra, -(-lines // TILE) * TILE), lanes), f32),
             pltpu.VMEM((CB, lines, LANES), f32),
             pltpu.VMEM((devices, lines, LANES), f32),
             pltpu.VMEM((TILE, atoms), f32),
-            pltpu.VMEM((2, TILE, ghosts), f32),
-            pltpu.VMEM((2, TILE, ghosts), f32),
+            pltpu.VMEM((2, 4, ghosts), f32),
+            pltpu.VMEM((2, 4, ghosts), f32),
             pltpu.VMEM((2, devices, piece_rows, LANES), f32),
             pltpu.VMEM((2, 4 * ghost_tiles * TILE, ghosts), f32),
             pltpu.VMEM((2, 4 * ghost_tiles * TILE, ghosts), f32),

time: 37.5 us -> 36.9 us (0.984)
  Pallas kernels: 36.1 us -> 35.4 us
    pallas_call x1, Pallas kernels: 36.1 us -> 35.4 us  [body(): pl.pallas_call(cycle_kernel, name='cycle', out_shape=shape, in_specs=[hbm...]
where the time goes in v4:
time: 36.9 us; the launch traced here: 36.7 us
  Pallas kernels  35.4 us (96%)
  between operations  0.64 us (2%)
  local copies, waits for them, and re-layouts  0.62 us (2%)
    pallas_call x1, Pallas kernels, body(): pl.pallas_call(cycle_kernel, name='cycle', out_shape=shape, in_specs=[hbm...  35.4 us

profile of v4, /device:TPU:0, one launch (start us, length us, event | category | flops | bytes accessed | tf_op | source)
XLA Modules:
  0.0 36.7 jit_solution(12788462525209849527)
XLA Ops:
  0.6 35.4 %cycle.1 = f32[2,3,4,512]{3,2,1,0:T(4,128)S(1)} custom-call(f32[3,4,512]{2,1,0:T(4,128)} %bitcast.15, f32[3,4,512]{2,1,0:T(4,128)} %bitcast.16, s32[32,512]{1,0:T(8,128)} %near_in.1, s32[2,128]{1,0:T(2,128)} %bitcast.19, s32[1,512]{1,0:T(1,128)} %bitcast.18, f32[1,2]{1,0:T(1,128)} %bitcast.20, f32[1,2]{1,0:T(1,128)} %bitcast.21, f32[8,128]{1,0:T(8,128)} %bitcast.17, ...), custom_call_target="tpu_custom_call" | custom-call | tf_op jit(solution)/shard_map/cycle/pallas_call | solution.py:741
  36.1 0.6 %slice_bitcast_fusion = (f32[4,3,512]{2,0,1:T(4,128)}, f32[4,3,512]{2,0,1:T(4,128)}) fusion(f32[2,3,4,512]{3,2,1,0:T(4,128)S(1)} %cycle.1), kind=kLoop, calls=%fused_computation | loop fusion | bytes 98304 | tf_op jit(solution)/shard_map/transpose | solution.py:787

commit v5 on v4

--- a/solution.py
+++ b/solution.py
@@ -194,13 +194,14 @@
     width = devices * TILE
     extra = halves * CB
 
+    steps = {}
+    bit = 1
+    while bit < devices:
+        steps[bit] = bit - 2 * bit * lax.rem(lax.div(me, bit), 2)
+        bit *= 2
+
     def partner(j):
-        at, bit = me, 1
-        while bit < devices:
-            if j & bit:
-                at = at + bit - 2 * bit * lax.rem(at // bit, 2)
-            bit *= 2
-        return at
+        return sum((steps[bit] for bit in steps if j & bit), me)
 
     peers = [partner(j) for j in range(devices)]
     order = list(range(devices - 1, 0, -1))
@@ -214,13 +215,13 @@
         pltpu.make_async_copy(src, dst, load_s.at[number])
         for number, (src, dst) in enumerate(pairs)
     ]
+    barrier = pltpu.get_barrier_semaphore()
+    for target in (above, below):
+        pl.semaphore_signal(barrier, inc=1, device_id={"space": target}, device_id_type=MESH)
+    for j in order:
+        pl.semaphore_signal(barrier, inc=1, device_id={"bead": peers[j]}, device_id_type=MESH)
     for load in loads:
         load.start()
-    barrier = pltpu.get_barrier_semaphore()
-    for j in order:
-        pl.semaphore_signal(barrier, inc=1, device_id={"bead": peers[j]}, device_id_type=MESH)
-    for target in (above, below):
-        pl.semaphore_signal(barrier, inc=1, device_id={"space": target}, device_id_type=MESH)
 
     ghost_at, part_at, begin_at, qghost_at, free_at, side_at = range(6)
     piece_at, kick_at, edge_at = 6, 8, 8 + NINNER
@@ -343,8 +344,8 @@
                 part_out[c, at : at + 1, :] = part_line[row : row + 1, lane_of(s, i)]
 
     pl.semaphore_wait(barrier, devices + 1)
+    send_peers(lambda j: part_out.at[lax.div(peers[j], groups)], part_in.at[me], part_at)
     send_sides(zg_out, zg_in, ghost_at)
-    send_peers(lambda j: part_out.at[peers[j] // groups], part_in.at[me], part_at)
     send_peers(lambda j: begin.at[me], begin.at[me], begin_at)
 
     for h in range(halves):

time: 36.9 us -> 36.8 us (level)
  no operation moved by 1% of the time
where the time goes in v5:
time: 36.8 us; the launch traced here: 36.6 us
  Pallas kernels  35.3 us (96%)
  between operations  0.64 us (2%)
  local copies, waits for them, and re-layouts  0.62 us (2%)
    pallas_call x1, Pallas kernels, body(): pl.pallas_call(cycle_kernel, name='cycle', out_shape=shape, in_specs=[hbm...  35.3 us

profile of v5, /device:TPU:0, one launch (start us, length us, event | category | flops | bytes accessed | tf_op | source)
XLA Modules:
  0.0 36.6 jit_solution(9158864978451540165)
XLA Ops:
  0.6 35.3 %cycle.1 = f32[2,3,4,512]{3,2,1,0:T(4,128)S(1)} custom-call(f32[3,4,512]{2,1,0:T(4,128)} %bitcast.15, f32[3,4,512]{2,1,0:T(4,128)} %bitcast.16, s32[32,512]{1,0:T(8,128)} %near_in.1, s32[2,128]{1,0:T(2,128)} %bitcast.19, s32[1,512]{1,0:T(1,128)} %bitcast.18, f32[1,2]{1,0:T(1,128)} %bitcast.20, f32[1,2]{1,0:T(1,128)} %bitcast.21, f32[8,128]{1,0:T(8,128)} %bitcast.17, ...), custom_call_target="tpu_custom_call" | custom-call | tf_op jit(solution)/shard_map/cycle/pallas_call | solution.py:742
  36.0 0.6 %slice_bitcast_fusion = (f32[4,3,512]{2,0,1:T(4,128)}, f32[4,3,512]{2,0,1:T(4,128)}) fusion(f32[2,3,4,512]{3,2,1,0:T(4,128)S(1)} %cycle.1), kind=kLoop, calls=%fused_computation | loop fusion | bytes 98304 | tf_op jit(solution)/shard_map/transpose | solution.py:788
